TPU v7x, 512 devices: a whole 4x4x16 slice. The times are simulated.
512 devices in a mesh: vocab: 16 (over z_hi, x, core), seq: 32 (over z_lo, y).
Axes of the slice: x: 4, y: 4, z: 16 (z_hi: 2, z_lo: 8; z = z_hi * 8 + z_lo), core: 2. Of those that a mesh axis runs over, the one named last changes fastest.
Arguments:
- token_ids: int32 [2, 2048], P(None, 'seq'), may hold values from 0 to 131071
- keep_mask: int32 [2, 2048], P(None, 'seq'), may hold values 0 or 1
- target_length: int32 [2], replicated, may hold values from 256 to 2048, as said below
- source_length: int32 [2], replicated, may hold values from 128 to 1024, as said below
- embed_table: bfloat16 [131072, 4096], P('vocab', 'seq'), may hold values from -6 to 6
- self_gain: float32 [4096], replicated, may hold values from 0.1 to 1.9
- query_weight: bfloat16 [4096, 2048], P('seq', 'vocab'), may hold values from -0.03125 to 0.03125
- key_weight: bfloat16 [4096, 2048], P('seq', 'vocab'), may hold values from -6 to 6
- value_weight: bfloat16 [4096, 2048], P('seq', 'vocab'), may hold values from -0.09375 to 0.09375
- self_out_weight: bfloat16 [2048, 4096], P('vocab'), may hold values from -0.5 to 0.5
- cross_gain: float32 [4096], replicated, may hold values from 0.1 to 1.9
- cross_query_weight: bfloat16 [4096, 2048], P('seq', 'vocab'), may hold values from -0.03125 to 0.03125
- cross_keys: bfloat16 [2, 1024, 2048], P(None, 'seq', 'vocab'), may hold values from -24 to 24
- cross_values: bfloat16 [2, 1024, 2048], P(None, 'seq', 'vocab'), may hold values from -6 to 6
- cross_out_weight: bfloat16 [2048, 4096], P('vocab'), may hold values from -0.375 to 0.375
Outputs:
- layer_output: bfloat16 [2, 2048, 4096], P(None, 'seq', 'vocab')
Inputs may be any that keep to these rules, and one draw needn't show every extreme that they name: `target_length`: the pairs' lengths all differ, and one pair has length 2048. `source_length`: the pairs' lengths all differ, and one pair has length 1024.
All inputs are finite; a program needn't handle non-finite values. No bound on the sum of `keep_mask` on one device may be relied on, other than what follows from the above.
Results may differ from a plain program's by a relative error of at most 0.035.
Values may be sent and summed in bfloat16 or wider, within the bound.
A program may use at most 64 MiB of HBM per device.

v0:
```python
import jax
import jax.numpy as jnp
from jax import lax
from jax.sharding import PartitionSpec as P

DH = 64


def rms_scale(values, gain):
    return values * lax.rsqrt(jnp.mean(values * values, axis=-1, keepdims=True) + 1e-06) * gain


def attend(query, keys, values, visible):
    pair_count = query.shape[0]
    query_rows = query.shape[1]
    head_count = query.shape[2] // DH
    q_heads = query.reshape(pair_count, query_rows, head_count, DH)
    k_heads = keys.reshape(pair_count, keys.shape[1], head_count, DH)
    v_heads = values.reshape(pair_count, values.shape[1], head_count, DH)
    scores = jnp.einsum("pqhd,pkhd->phqk", q_heads, k_heads, preferred_element_type=jnp.float32)
    scores = jnp.where(visible[:, None, :, :], scores, -jnp.inf)
    raised = jnp.exp(scores - jnp.max(scores, axis=-1, keepdims=True))
    totals = jnp.sum(raised, axis=-1)
    mixed = jnp.einsum(
        "phqk,pkhd->pqhd", raised.astype(jnp.bfloat16), v_heads, preferred_element_type=jnp.float32
    )
    mixed = mixed / jnp.transpose(totals, (0, 2, 1))[:, :, :, None]
    return mixed.reshape(pair_count, query_rows, head_count * DH).astype(jnp.bfloat16)


def row_fold(source, portion):
    return jnp.dot(source, portion, preferred_element_type=jnp.float32)


def on_device(
    token_ids,
    keep_mask,
    target_length,
    source_length,
    embed_table,
    self_gain,
    query_weight,
    key_weight,
    value_weight,
    self_out_weight,
    cross_gain,
    cross_query_weight,
    cross_keys,
    cross_values,
    cross_out_weight,
):
    seq_count = lax.axis_size("seq")
    seq_index = lax.axis_index("seq")
    vocab_index = lax.axis_index("vocab")
    vocab_count = lax.axis_size("vocab")
    every_id = lax.all_gather(token_ids, "seq", axis=1, tiled=True)
    shard_rows = embed_table.shape[0]
    local_ids = every_id - vocab_index * shard_rows
    inside = (local_ids >= 0) & (local_ids < shard_rows)
    picked = jnp.take(embed_table, jnp.clip(local_ids, 0, shard_rows - 1).reshape(-1), axis=0)
    picked = picked.reshape(every_id.shape[0], every_id.shape[1], embed_table.shape[1])
    partial_rows = jnp.where(inside[:, :, None], picked, jnp.zeros_like(picked))
    arrived = lax.all_to_all(partial_rows, "seq", split_axis=1, concat_axis=2, tiled=True)
    summed = lax.psum(arrived.astype(jnp.float32).astype(jnp.bfloat16), "vocab").astype(jnp.float32)
    embedded_pairs = summed * keep_mask.astype(jnp.float32)[:, :, None]
    pair_count = embedded_pairs.shape[0]
    token_rows = embedded_pairs.shape[1]
    model_cols = embedded_pairs.shape[2]
    flat_rows = pair_count * token_rows
    embedded = embedded_pairs.reshape(flat_rows, model_cols)
    self_normed = rms_scale(embedded, self_gain).astype(jnp.bfloat16)
    queries = row_fold(self_normed, lax.all_gather(query_weight, "seq", axis=0, tiled=True))
    keys = row_fold(self_normed, lax.all_gather(key_weight, "seq", axis=0, tiled=True))
    values = row_fold(self_normed, lax.all_gather(value_weight, "seq", axis=0, tiled=True))
    head_cols = queries.shape[1]
    queries = queries.astype(jnp.bfloat16).reshape(pair_count, token_rows, head_cols)
    keys = keys.astype(jnp.bfloat16).reshape(pair_count, token_rows, head_cols)
    values = values.astype(jnp.bfloat16).reshape(pair_count, token_rows, head_cols)
    keys_every, values_every = (
        lax.all_gather(keys, "seq", axis=1, tiled=True),
        lax.all_gather(values, "seq", axis=1, tiled=True),
    )
    query_pos = seq_index * token_rows + jnp.arange(token_rows, dtype=jnp.int32)
    key_pos = jnp.arange(token_rows * seq_count, dtype=jnp.int32)
    causal = key_pos[None, :] <= query_pos[:, None]
    visible = causal[None, :, :] & (key_pos[None, None, :] < target_length[:, None, None])
    self_context = attend(queries, keys_every, values_every, visible).reshape(flat_rows, head_cols)
    self_terms = jnp.dot(self_context, self_out_weight, preferred_element_type=jnp.float32)
    share_cols = model_cols // vocab_count
    col_start = vocab_index * share_cols
    after_self = embedded + lax.psum(self_terms.astype(jnp.bfloat16), "vocab").astype(jnp.float32)
    cross_normed = rms_scale(after_self, cross_gain).astype(jnp.bfloat16)
    after_share = lax.dynamic_slice_in_dim(after_self, col_start, share_cols, 1)
    cross_queries = row_fold(
        cross_normed, lax.all_gather(cross_query_weight, "seq", axis=0, tiled=True)
    )
    cross_queries = cross_queries.astype(jnp.bfloat16).reshape(pair_count, token_rows, head_cols)
    source_keys, source_values = (
        lax.all_gather(cross_keys, "seq", axis=1, tiled=True),
        lax.all_gather(cross_values, "seq", axis=1, tiled=True),
    )
    source_pos = jnp.arange(source_keys.shape[1], dtype=jnp.int32)
    cross_visible = jnp.broadcast_to(
        source_pos[None, None, :] < source_length[:, None, None],
        (pair_count, token_rows, source_keys.shape[1]),
    )
    cross_context = attend(cross_queries, source_keys, source_values, cross_visible).reshape(
        flat_rows, head_cols
    )
    cross_terms = jnp.dot(cross_context, cross_out_weight, preferred_element_type=jnp.float32)
    cross_share = lax.psum_scatter(
        cross_terms.astype(jnp.bfloat16), "vocab", scatter_dimension=1, tiled=True
    ).astype(jnp.float32)
    return (
        (after_share + cross_share).reshape(pair_count, token_rows, share_cols).astype(jnp.bfloat16)
    )


def solution(mesh):
    return jax.shard_map(
        on_device,
        mesh=mesh,
        in_specs=(
            P(None, "seq"),
            P(None, "seq"),
            P(),
            P(),
            P("vocab", "seq"),
            P(),
            P("seq", "vocab"),
            P("seq", "vocab"),
            P("seq", "vocab"),
            P("vocab", None),
            P(),
            P("seq", "vocab"),
            P(None, "seq", "vocab"),
            P(None, "seq", "vocab"),
            P("vocab", None),
        ),
        out_specs=P(None, "seq", "vocab"),
        check_vma=False,
    )
```

profile of v0, /device:TPU:480, one launch (start us, length us, event | category | flops | bytes accessed | tf_op | source)
XLA Modules:
  0.0 1690.9 jit_solution(9061207319396813482)
XLA Ops:
  7.4 98.9 %all-gather = s32[32,64,2]{1,2,0:T(2,128)S(1)} all-gather(s32[1,64,2]{1,2,0:T(2,128)} %bitcast.79), channel_id=1, replica_groups=mesh['vocab'=16,'seq'=32] {'seq'}, dimensions={0}, use_global_device_ids=true | all-gather | bytes 16896 | tf_op jit(solution)/shard_map/all_gather | solution.py:56
  107.1 1.1 copy.49
  108.2 12.1 gather_fusion
  120.3 10.4 broadcast_select_fusion.1
  130.8 59.5 %all_to_all.18 = bf16[2,2048,128]{2,0,1:T(2,128)(2,1)S(1)} all-to-all(bf16[2,2048,128]{2,0,1:T(2,128)(2,1)S(1)} %broadcast_select_fusion.1), channel_id=1, replica_groups=mesh['vocab'=16,'seq'=32] {'seq'}, dimensions={1} | all-to-all | bytes 2097152 | tf_op jit(solution)/shard_map/all_to_all | solution.py:63
  190.2 0.7 copy.52
  190.9 1.3 all_to_all.16
  194.1 255.9 %all-reduce.3.cloned.1.call-done = bf16[2,64,4096]{2,1,0:T(8,128)(2,1)} async-done(((bf16[2,64,4096]{2,1,0:T(8,128)(2,1)}), bf16[2,64,4096]{2,1,0:T(8,128)(2,1)}) %all-reduce.3.cloned.1.call-update) | async-done | bytes 1048592 | tf_op jit(solution)/shard_map/psum | solution.py:64
  449.9 2.9 multiply_reduce_fusion.1
  452.9 1.9 fusion.1
  454.8 2.2 convolution_convert_fusion.3
  457.2 169.6 %all-gather.8.cloned.1.call-done = bf16[4096,128]{1,0:T(8,128)(2,1)} async-done(((bf16[128,128]{1,0:T(8,128)(2,1)}), bf16[4096,128]{1,0:T(8,128)(2,1)}) %all-gather.8.cloned.1.call-update) | async-done | bytes 1048592 | tf_op jit(solution)/shard_map/all_gather | solution.py:74
  626.8 2.3 convolution_convert_fusion.5
  629.5 219.2 %all-gather.12.cloned.1.call-done = bf16[4096,128]{1,0:T(8,128)(2,1)} async-done(((bf16[128,128]{1,0:T(8,128)(2,1)}), bf16[4096,128]{1,0:T(8,128)(2,1)}) %all-gather.12.cloned.1.call-update) | async-done | bytes 1048592 | tf_op jit(solution)/shard_map/all_gather | solution.py:72
  848.7 1.6 convolution_convert_fusion.4
  850.5 220.5 %all-gather.16.cloned.1.call-done = bf16[2,2048,128]{2,1,0:T(8,128)(2,1)} async-done(((bf16[2,64,128]{2,1,0:T(8,128)(2,1)}), bf16[2,2048,128]{2,1,0:T(8,128)(2,1)}) %all-gather.16.cloned.1.call-update) | async-done | bytes 1048592 | tf_op jit(solution)/shard_map/all_gather | solution.py:80
  1070.9 1.5 copy.54
  1073.0 1.3 copy-done.1
  1074.8 218.4 %all-gather.10.cloned.1.call-done = bf16[2,2048,128]{2,1,0:T(8,128)(2,1)} async-done(((bf16[2,64,128]{2,1,0:T(8,128)(2,1)}), bf16[2,2048,128]{2,1,0:T(8,128)(2,1)}) %all-gather.10.cloned.1.call-update) | async-done | bytes 1048592 | tf_op jit(solution)/shard_map/all_gather | solution.py:81
  1293.1 1.5 copy.53
  1294.6 2.1 fusion.7
  1296.9 2.6 convolution_convert_fusion.1
  1299.7 0.7 all-gather.18.cloned.1.call-update
  1300.4 114.4 %all_gather.34 = bf16[2,1024,128]{2,1,0:T(8,128)(2,1)S(1)} all-gather(bf16[2,32,128]{2,1,0:T(8,128)(2,1)S(1)} %copy-done.6), channel_id=1, replica_groups=mesh['vocab'=16,'seq'=32] {'seq'}, dimensions={1}, use_global_device_ids=true | all-gather | bytes 540672 | tf_op jit(solution)/shard_map/all_gather | solution.py:99
  1415.0 118.3 %all_gather.35 = bf16[2,1024,128]{2,1,0:T(8,128)(2,1)S(1)} all-gather(bf16[2,32,128]{2,1,0:T(8,128)(2,1)S(1)} %copy-done.7), channel_id=1, replica_groups=mesh['vocab'=16,'seq'=32] {'seq'}, dimensions={1}, use_global_device_ids=true | all-gather | bytes 540672 | tf_op jit(solution)/shard_map/all_gather | solution.py:100
  1533.3 1.0 copy.59
  1534.4 34.9 %all-reduce.5.cloned.1.call-done = bf16[128,4096]{1,0:T(8,128)(2,1)} async-done(((bf16[128,4096]{1,0:T(8,128)(2,1)}), bf16[128,4096]{1,0:T(8,128)(2,1)}) %all-reduce.5.cloned.1.call-update) | async-done | bytes 1048592 | tf_op jit(solution)/shard_map/psum | solution.py:91
  1569.4 3.5 multiply_reduce_fusion
  1572.9 2.3 convolution_convert_fusion.2
  1577.0 1.4 convolution_convert_fusion
  1578.4 103.7 %reduce-scatter.2.cloned.1.call-done = bf16[128,256]{1,0:T(8,128)(2,1)} async-done(((bf16[128,4096]{1,0:T(8,128)(2,1)}), bf16[128,256]{1,0:T(8,128)(2,1)}) %reduce-scatter.2.cloned.1.call-update) | async-done | bytes 65552 | tf_op jit(solution)/shard_map/reduce_scatter | solution.py:111
  1682.2 1.6 add_convert_fusion
  (70 shorter events, 6.6 us)
Async XLA Ops:
  7.4 100.8 %copy-start = (bf16[8192,128]{1,0:T(8,128)(2,1)S(1)}, bf16[8192,128]{1,0:T(8,128)(2,1)}, u32[]{:S(2)}) copy-start(bf16[8192,128]{1,0:T(8,128)(2,1)} %param.19) | copy-start | bytes 6291460
  7.4 442.6 %all-reduce.3.cloned.1.call-start = ((), (), s32[]{:S(2)}) async-start(), calls=%async_computation.2 | async-start | bytes 2097152 | tf_op jit(solution)/shard_map/psum | solution.py:64
  190.9 3.1 copy-start.8
  192.2 260.7 %copy-start.4 = (f32[4096]{0:T(1024)S(1)}, f32[4096]{0:T(1024)}, u32[]{:S(2)}) copy-start(f32[4096]{0:T(1024)} %param.20) | copy-start | bytes 49156
  192.2 262.6 %all-gather.14.cloned.1.call-start = ((), (), s32[]{:S(2)}) async-start(), calls=%async_computation.6 | async-start | bytes 1081344 | tf_op jit(solution)/shard_map/all_gather | solution.py:73
  192.8 433.9 %all-gather.8.cloned.1.call-start = ((), (), s32[]{:S(2)}) async-start(), calls=%async_computation.3 | async-start | bytes 1081344 | tf_op jit(solution)/shard_map/all_gather | solution.py:74
  193.4 655.3 %all-gather.12.cloned.1.call-start = ((), (), s32[]{:S(2)}) async-start(), calls=%async_computation.5 | async-start | bytes 1081344 | tf_op jit(solution)/shard_map/all_gather | solution.py:72
  194.0 876.9 %all-gather.16.cloned.1.call-start = ((), (), s32[]{:S(2)}) async-start(), calls=%async_computation.7 | async-start | bytes 1081344 | tf_op jit(solution)/shard_map/all_gather | solution.py:80
  454.8 174.3 %copy-start.9 = (s32[2]{0:T(128)S(1)}, s32[2]{0:T(128)}, u32[]{:S(2)}) copy-start(s32[2]{0:T(128)} %param.17) | copy-start | bytes 28
  457.1 836.0 %all-gather.10.cloned.1.call-start = ((), (), s32[]{:S(2)}) async-start(), calls=%async_computation.4 | async-start | bytes 1081344 | tf_op jit(solution)/shard_map/all_gather | solution.py:81
  629.1 940.3 %all-reduce.5.cloned.1.call-start = ((), (), s32[]{:S(2)}) async-start(), calls=%async_computation.8 | async-start | bytes 2097152 | tf_op jit(solution)/shard_map/psum | solution.py:91
  1073.0 1.3 copy-start.1
  1296.7 3.7 copy-start.6
  1296.9 118.1 %copy-start.7 = (bf16[2,32,128]{2,1,0:T(8,128)(2,1)S(1)}, bf16[2,32,128]{2,1,0:T(8,128)(2,1)}, u32[]{:S(2)}) copy-start(bf16[2,32,128]{2,1,0:T(8,128)(2,1)} %param.28) | copy-start | bytes 49156
  1299.6 234.8 %copy-start.10 = (s32[2]{0:T(128)S(1)}, s32[2]{0:T(128)}, u32[]{:S(2)}) copy-start(s32[2]{0:T(128)} %param.18) | copy-start | bytes 28
  1299.6 273.3 %all-gather.18.cloned.1.call-start = ((), (), s32[]{:S(2)}) async-start(), calls=%async_computation.9 | async-start | bytes 1081344 | tf_op jit(solution)/shard_map/all_gather | solution.py:95
  1300.3 381.8 %reduce-scatter.2.cloned.1.call-start = ((), (), s32[]{:S(2)}) async-start(), calls=%async_computation.10 | async-start | bytes 1114112 | tf_op jit(solution)/shard_map/reduce_scatter | solution.py:111
  1534.4 38.5 %copy-start.5 = (f32[4096]{0:T(1024)S(1)}, f32[4096]{0:T(1024)}, u32[]{:S(2)}) copy-start(f32[4096]{0:T(1024)} %param.25) | copy-start | bytes 49156
  1575.4 1.0 copy-start.3
  1575.7 1.3 copy-start.2
Sparse Core Ops, SparseCore 0:
  192.4 257.5 all-reduce.2
  1299.7 269.5 all-reduce.4
  1578.5 103.5 reduce-scatter.1
Sparse Core Ops, SparseCore 1:
  194.8 210.1 all-gather.13
  406.9 219.8 all-gather.7
  628.7 219.9 all-gather.11
  850.8 220.0 all-gather.15
  1073.0 220.0 all-gather.9
  1302.5 220.8 all-gather.17
where the time goes:
time: 1700 us; the launch traced here: 1690 us
  waiting for transfers between devices  1220 us (72%)
  blocking collectives  391 us (23%)
  local copies, waits for them, and re-layouts  22.4 us (1%)
  other arithmetic  21.6 us (1%)
    psum x1, waiting for transfers between devices, on_device(): lax.psum(arrived.astype(jnp.float32).astype(jnp.bfloat16), 'vocab')  256 us
    all_gather x1, waiting for transfers between devices, on_device(): lax.all_gather(keys, 'seq', axis=1, tiled=True)  220 us
    all_gather x1, waiting for transfers between devices, on_device(): lax.all_gather(query_weight, 'seq', axis=0, tiled=True)  219 us
    all_gather x1, waiting for transfers between devices, on_device(): lax.all_gather(values, 'seq', axis=1, tiled=True)  218 us
    all_gather x1, waiting for transfers between devices, on_device(): lax.all_gather(value_weight, 'seq', axis=0, tiled=True)  170 us
    all_gather x1, blocking collectives, on_device(): lax.all_gather(cross_values, 'seq', axis=1, tiled=True)  118 us
    all_gather x1, blocking collectives, on_device(): lax.all_gather(cross_keys, 'seq', axis=1, tiled=True)  114 us
    reduce_scatter x1, waiting for transfers between devices, on_device(): lax.psum_scatter(cross_terms.astype(jnp.bfloat16), 'vocab', scatter_dimen...  104 us
  transfers between devices with their start and end apart: 9, of which 7 were waited for; matrix products, arithmetic and copies ran while one was open for 1% of the time, Pallas kernels for 0%

commit v1 on v0

v1 whole, which is shorter than its diff:
```python
import functools

import jax
import jax.numpy as jnp
from jax import lax
from jax.experimental import pallas as pl
from jax.experimental.pallas import tpu as pltpu
from jax.sharding import PartitionSpec as P

DH = 64
MESH = pl.DeviceIdType.MESH
F32 = jnp.float32
BF16 = jnp.bfloat16

LINE_Y = ("seq", 4, 1)
LINE_Z = ("seq", 8, 4)
LINE_CORE = ("vocab", 2, 1)
LINE_X = ("vocab", 4, 2)
LINE_ZH = ("vocab", 2, 8)


def place_on(line):
    axis, members, stride = line
    return lax.rem(lax.axis_index(axis) // stride, members)


def peer_of(line, shift):
    axis, members, stride = line
    here = lax.axis_index(axis)
    mine = lax.rem(here // stride, members)
    other = lax.rem(mine + shift, members)
    there = here + (other - mine) * stride
    if axis == "seq":
        return (lax.axis_index("vocab"), there), other
    return (there, lax.axis_index("seq")), other


def push_kernel(line, gather, x_ref, o_ref, own_sem, send_sem, recv_sem):
    members = line[1]
    mine = place_on(line)
    barrier = pltpu.get_barrier_semaphore()
    for shift in range(1, members):
        target, _ = peer_of(line, shift)
        pl.semaphore_signal(barrier, inc=1, device_id=target, device_id_type=MESH)
    own = pltpu.make_async_copy(x_ref if gather else x_ref.at[mine], o_ref.at[mine], own_sem)
    own.start()
    pl.semaphore_wait(barrier, members - 1)
    copies = []
    for shift in range(1, members):
        target, other = peer_of(line, shift)
        copy = pltpu.make_async_remote_copy(
            src_ref=x_ref if gather else x_ref.at[other],
            dst_ref=o_ref.at[mine],
            send_sem=send_sem.at[shift - 1],
            recv_sem=recv_sem.at[shift - 1],
            device_id=target,
            device_id_type=MESH,
        )
        copy.start()
        copies.append(copy)
    own.wait()
    for copy in copies:
        copy.wait()


def push(x, line, ident, gather):
    members = line[1]
    shape = ((members,) + x.shape) if gather else x.shape
    return pl.pallas_call(
        functools.partial(push_kernel, line, gather),
        out_shape=jax.ShapeDtypeStruct(shape, x.dtype),
        in_specs=[pl.BlockSpec(memory_space=pltpu.VMEM)],
        out_specs=pl.BlockSpec(memory_space=pltpu.VMEM),
        scratch_shapes=[
            pltpu.SemaphoreType.DMA,
            pltpu.SemaphoreType.DMA((members - 1,)),
            pltpu.SemaphoreType.DMA((members - 1,)),
        ],
        compiler_params=pltpu.CompilerParams(collective_id=ident, has_side_effects=True),
    )(x)


def relay_kernel(line, x_ref, o_ref, own_sem, up_send, up_recv, down_send, down_recv):
    members = line[1]
    mine = place_on(line)
    barrier = pltpu.get_barrier_semaphore()
    up, _ = peer_of(line, 1)
    down, _ = peer_of(line, members - 1)
    has_up = mine < members - 1
    has_down = mine > 0

    @pl.when(has_up)
    def _():
        pl.semaphore_signal(barrier, inc=1, device_id=up, device_id_type=MESH)

    @pl.when(has_down)
    def _():
        pl.semaphore_signal(barrier, inc=1, device_id=down, device_id_type=MESH)

    own = pltpu.make_async_copy(x_ref, o_ref.at[mine], own_sem)
    own.start()

    @pl.when(has_up & has_down)
    def _():
        pl.semaphore_wait(barrier, 2)

    @pl.when(jnp.logical_not(has_up & has_down))
    def _():
        pl.semaphore_wait(barrier, 1)

    def make(source, target, step, sends, recvs):
        return pltpu.make_async_remote_copy(
            src_ref=x_ref if step == 1 else o_ref.at[source],
            dst_ref=o_ref.at[source],
            send_sem=sends.at[step - 1],
            recv_sem=recvs.at[step - 1],
            device_id=target,
            device_id_type=MESH,
        )

    for step in range(1, members):
        rising = mine - (step - 1)
        falling = mine + (step - 1)

        @pl.when(has_up & (rising >= 0))
        def _():
            make(rising, up, step, up_send, up_recv).start()

        @pl.when(has_down & (falling < members))
        def _():
            make(falling, down, step, down_send, down_recv).start()

        @pl.when(mine - step >= 0)
        def _():
            make(mine - step, up, step, up_send, up_recv).wait_recv()

        @pl.when(mine + step < members)
        def _():
            make(mine + step, down, step, down_send, down_recv).wait_recv()

    for step in range(1, members):

        @pl.when(has_up & (mine - (step - 1) >= 0))
        def _():
            make(mine - (step - 1), up, step, up_send, up_recv).wait_send()

        @pl.when(has_down & (mine + (step - 1) < members))
        def _():
            make(mine + (step - 1), down, step, down_send, down_recv).wait_send()

    own.wait()


def relay(x, line, ident):
    members = line[1]
    sems = pltpu.SemaphoreType.DMA((members - 1,))
    return pl.pallas_call(
        functools.partial(relay_kernel, line),
        out_shape=jax.ShapeDtypeStruct((members,) + x.shape, x.dtype),
        in_specs=[pl.BlockSpec(memory_space=pltpu.VMEM)],
        out_specs=pl.BlockSpec(memory_space=pltpu.VMEM),
        scratch_shapes=[pltpu.SemaphoreType.DMA, sems, sems, sems, sems],
        compiler_params=pltpu.CompilerParams(collective_id=ident, has_side_effects=True),
    )(x)


def fold(blocks):
    return jnp.sum(blocks.astype(F32), axis=0)


def scatter_sum(x, ident):
    x = fold(push(x, LINE_CORE, ident, False)).astype(BF16)
    x = fold(push(x, LINE_X, ident + 1, False)).astype(BF16)
    return fold(push(x, LINE_ZH, ident + 2, False))


def spread(x, ident):
    x = push(x, LINE_ZH, ident, True)
    x = push(x, LINE_X, ident + 1, True)
    return push(x, LINE_CORE, ident + 2, True)


def split_sum(values):
    high = values.astype(BF16)
    low = (values - high.astype(F32)).astype(BF16)
    return high, low


def attend(query, keys, values, visible):
    scores = lax.dot_general(query, keys, (((1,), (1,)), ((), ())), preferred_element_type=F32)
    scores = jnp.where(visible, scores, -jnp.inf)
    raised = jnp.exp(scores - jnp.max(scores, axis=-1, keepdims=True))
    totals = jnp.sum(raised, axis=-1, keepdims=True)
    mixed = jnp.dot(raised.astype(BF16), values, preferred_element_type=F32)
    return (mixed / totals).astype(BF16)


def on_device(
    token_ids,
    keep_mask,
    target_length,
    source_length,
    embed_table,
    self_gain,
    query_weight,
    key_weight,
    value_weight,
    self_out_weight,
    cross_gain,
    cross_query_weight,
    cross_keys,
    cross_values,
    cross_out_weight,
):
    pairs, tokens = token_ids.shape
    vocab_index = lax.axis_index("vocab")
    y_index = place_on(LINE_Y)
    z_index = place_on(LINE_Z)
    n_y, n_z, n_v = LINE_Y[1], LINE_Z[1], lax.axis_size("vocab")
    width = self_gain.shape[0]
    quarter = width // n_y
    cols = embed_table.shape[1]
    heads = 2
    row = n_y * tokens
    row_tokens = pairs * row
    piece = row_tokens // n_v

    ids = jnp.where(keep_mask != 0, token_ids, -1).reshape(1, pairs * tokens)
    ids = push(ids, LINE_Y, 0, True)
    ids = push(ids.reshape(n_y, pairs * tokens), LINE_Z, 1, True)
    ids = ids.reshape(n_z, n_y, pairs, tokens).transpose(0, 2, 1, 3)
    ids = ids.reshape(n_z, n_v, piece).transpose(1, 0, 2).reshape(-1)

    pos = cross_keys.shape[1]
    both = jnp.stack(
        [cross_keys.reshape(pairs, pos, heads, DH), cross_values.reshape(pairs, pos, heads, DH)], axis=3
    )
    both = both.transpose(0, 2, 1, 3, 4).reshape(n_y, pos, 2 * DH)
    both = push(both, LINE_Y, 2, False).reshape(n_y * pos, 2 * DH)
    weights = jnp.concatenate([query_weight, key_weight, value_weight, cross_query_weight, both], axis=1)
    weights = relay(weights, LINE_Z, 3)
    head_cols = query_weight.shape[1]
    weights = weights.reshape(n_z * cols, 4 * head_cols + 2 * DH)
    source_both = weights[:, 4 * head_cols :]

    shard_rows = embed_table.shape[0]
    local_ids = ids - vocab_index * shard_rows
    inside = (local_ids >= 0) & (local_ids < shard_rows)
    picked = jnp.take(embed_table, jnp.clip(local_ids, 0, shard_rows - 1), axis=0)
    picked = jnp.where(inside[:, None], picked, jnp.zeros_like(picked))
    own_rows = scatter_sum(picked.reshape(2, 4, 2, n_z * piece, cols), 4).astype(BF16)
    own_rows = push(own_rows.reshape(n_z, piece, cols), LINE_Z, 7, False)
    own_rows = own_rows.transpose(1, 0, 2).reshape(piece, quarter)
    embedded = spread(own_rows, 8).reshape(row_tokens, quarter)

    def part_of_gain(gain):
        return lax.dynamic_index_in_dim(gain.reshape(n_z, n_y, cols), y_index, 1, False).reshape(quarter)

    wide = embedded.astype(F32)
    squares = jnp.sum(wide * wide, axis=-1)
    scaled = (wide * part_of_gain(self_gain)).astype(BF16)
    partial = jnp.dot(scaled, weights[:, : 3 * head_cols], preferred_element_type=F32).astype(BF16)
    partial = partial.reshape(pairs, row, 3, heads, DH).transpose(0, 3, 1, 2, 4).reshape(n_y, row, 3 * DH)
    high, low = split_sum(squares.reshape(pairs, 1, row))

    def tail(count):
        ends = jnp.stack([high, low], axis=-1)
        ends = jnp.broadcast_to(ends, (pairs, heads, row, 2)).reshape(n_y, row, 2)
        return jnp.pad(ends, ((0, 0), (0, 0), (0, count - 2)))

    summed = fold(push(jnp.concatenate([partial, tail(DH)], axis=2), LINE_Y, 11, False))
    scale = lax.rsqrt((summed[:, 3 * DH] + summed[:, 3 * DH + 1]) / width + 1e-06)
    qkv = (summed[:, : 3 * DH] * scale[:, None]).astype(BF16)
    kv = relay(qkv[:, DH:], LINE_Z, 12).reshape(n_z * row, 2 * DH)

    pair = y_index // heads
    query_pos = z_index * row + lax.broadcasted_iota(jnp.int32, (row, n_z * row), 0)
    key_pos = lax.broadcasted_iota(jnp.int32, (row, n_z * row), 1)
    visible = (key_pos <= query_pos) & (key_pos < lax.dynamic_index_in_dim(target_length, pair, 0, False))
    context = attend(qkv[:, :DH], kv[:, :DH], kv[:, DH:], visible)
    context = push(jnp.pad(context, ((0, 0), (0, DH))), LINE_Y, 13, True)[:, :, :DH]
    context = context.reshape(pairs, heads, row, DH).transpose(0, 2, 1, 3).reshape(row_tokens, heads * DH)
    out_part = lax.dynamic_index_in_dim(self_out_weight.reshape(-1, n_z, n_y, cols), y_index, 2, False)
    terms = jnp.dot(context, out_part.reshape(-1, quarter), preferred_element_type=F32).astype(BF16)
    after = own_rows.astype(F32) + scatter_sum(terms.reshape(2, 4, 2, piece, quarter), 14)
    after = spread(after.astype(BF16), 17).reshape(row_tokens, quarter)

    wide = after.astype(F32)
    squares = jnp.sum(wide * wide, axis=-1)
    scaled = (wide * part_of_gain(cross_gain)).astype(BF16)
    partial = jnp.dot(
        scaled, weights[:, 3 * head_cols : 4 * head_cols], preferred_element_type=F32
    ).astype(BF16)
    partial = partial.reshape(pairs, row, heads, DH).transpose(0, 2, 1, 3).reshape(n_y, row, DH)
    high, low = split_sum(squares.reshape(pairs, 1, row))
    block = lax.dynamic_index_in_dim(after.reshape(row_tokens, n_z, cols), vocab_index // 2, 1, False)
    block = block.reshape(pairs, n_y, tokens, cols).transpose(1, 0, 2, 3).reshape(n_y, pairs * tokens, cols)
    message = jnp.concatenate([jnp.concatenate([partial, tail(DH)], axis=2), block], axis=1)
    message = push(message, LINE_Y, 20, False)
    summed = fold(message[:, :row])
    scale = lax.rsqrt((summed[:, DH] + summed[:, DH + 1]) / width + 1e-06)
    cross_queries = (summed[:, :DH] * scale[:, None]).astype(BF16)
    blocks = message[:, row:].reshape(2, 2, pairs * tokens, cols)
    residual = lax.dynamic_index_in_dim(blocks, lax.rem(vocab_index, 2), 0, False)
    residual = residual.transpose(1, 0, 2).reshape(pairs * tokens, 2 * cols)

    source_pos = lax.broadcasted_iota(jnp.int32, (row, source_both.shape[0]), 1)
    visible = source_pos < lax.dynamic_index_in_dim(source_length, pair, 0, False)
    context = attend(cross_queries, source_both[:, :DH], source_both[:, DH:], visible)
    context = push(jnp.pad(context, ((0, 0), (0, DH))).reshape(n_y, tokens, 2 * DH), LINE_Y, 21, False)
    context = context[:, :, :DH].reshape(pairs, heads, tokens, DH).transpose(0, 2, 1, 3)
    context = context.reshape(pairs * tokens, heads * DH)
    terms = jnp.dot(context, cross_out_weight, preferred_element_type=F32).astype(BF16)
    share = width // n_v
    terms = terms.reshape(pairs * tokens, 2, 4, 2, share).transpose(3, 2, 1, 0, 4)
    result = residual.astype(F32) + scatter_sum(terms, 22)
    return result.astype(BF16).reshape(pairs, tokens, share)


def solution(mesh):
    return jax.shard_map(
        on_device,
        mesh=mesh,
        in_specs=(
            P(None, "seq"),
            P(None, "seq"),
            P(),
            P(),
            P("vocab", "seq"),
            P(),
            P("seq", "vocab"),
            P("seq", "vocab"),
            P("seq", "vocab"),
            P("vocab", None),
            P(),
            P("seq", "vocab"),
            P(None, "seq", "vocab"),
            P(None, "seq", "vocab"),
            P("vocab", None),
        ),
        out_specs=P(None, "seq", "vocab"),
        check_vma=False,
    )
```

time: 1700 us -> 406 us (0.24)
  the two profiles are of different devices: /device:TPU:480 before, /device:TPU:1 now
where the time goes in v1:
time: 406 us; the launch traced here: 403 us
  Pallas kernels  320 us (79%)
  local copies, waits for them, and re-layouts  37.1 us (9%)
  other arithmetic  32.8 us (8%)
  matrix products  12.3 us (3%)
    pallas_call x23, Pallas kernels, push(): pl.pallas_call(functools.partial(push_kernel, line, gather), out_shape=ja...  254 us
    pallas_call x2, Pallas kernels, relay(): pl.pallas_call(functools.partial(relay_kernel, line), out_shape=jax.Shape...  66.2 us
    reduce_sum x11, other arithmetic, fold(): return jnp.sum(blocks.astype(F32), axis=0)  18.1 us
    gather x1, local copies, waits for them, and re-layouts, on_device(): jnp.take(embed_table, jnp.clip(local_ids, 0, shard_rows - 1), axis=0)  12.1 us

profile of v1, /device:TPU:1, one launch (start us, length us, event | category | flops | bytes accessed | tf_op | source)
XLA Modules:
  0.0 403.2 jit_solution(14709776637191643842)
XLA Ops:
  2.2 7.7 %shard_map.145 = s32[4,1,128]{2,1,0:T(1,128)} custom-call(s32[1,128]{1,0:T(1,128)} %reshape.280.x_ref), custom_call_target="tpu_custom_call" | custom-call | tf_op jit(solution)/shard_map/pallas_call | solution.py:69
  9.9 14.6 %shard_map.146 = s32[8,4,128]{2,1,0:T(4,128)} custom-call(s32[4,128]{1,0:T(4,128)} %bitcast.134), custom_call_target="tpu_custom_call" | custom-call | tf_op jit(solution)/shard_map/pallas_call | solution.py:69
  25.7 12.1 %gather_fusion = bf16[4096,128]{1,0:T(8,128)(2,1)S(1)} fusion(bf16[8192,128]{1,0:T(8,128)(2,1)S(1)} %copy-done, s32[4096]{0:T(1024)S(1)} %broadcast_clamp_fusion), kind=kCustom, calls=%fused_computation | custom fusion | bytes 2113536 | tf_op jit(solution)/shard_map/jit(_take)/gather | solution.py:249
  38.3 2.5 select_select_fusion.x_ref
  40.8 8.4 %shard_map.147 = bf16[2,4,2,256,128]{4,3,2,1,0:T(8,128)(2,1)} custom-call(bf16[2,4,2,256,128]{4,3,2,1,0:T(8,128)(2,1)} %select_select_fusion.x_ref), custom_call_target="tpu_custom_call" | custom-call | tf_op jit(solution)/shard_map/pallas_call | solution.py:69
  49.1 2.4 reduce_sum.158.x_ref
  51.5 11.6 %shard_map.148 = bf16[4,2,256,128]{3,2,1,0:T(8,128)(2,1)} custom-call(bf16[4,2,256,128]{3,2,1,0:T(8,128)(2,1)} %reduce_sum.158.x_ref), custom_call_target="tpu_custom_call" | custom-call | tf_op jit(solution)/shard_map/pallas_call | solution.py:69
  64.9 14.4 %shard_map.149 = bf16[2,256,128]{2,1,0:T(8,128)(2,1)} custom-call(bf16[2,256,128]{2,1,0:T(8,128)(2,1)} %reduce_sum.159.x_ref), custom_call_target="tpu_custom_call" | custom-call | tf_op jit(solution)/shard_map/pallas_call | solution.py:69
  80.8 15.7 %shard_map.150 = bf16[8,32,128]{2,1,0:T(8,128)(2,1)} custom-call(bf16[8,32,128]{2,1,0:T(8,128)(2,1)} %bitcast.122), custom_call_target="tpu_custom_call" | custom-call | tf_op jit(solution)/shard_map/pallas_call | solution.py:69
  98.1 14.3 %shard_map.151.x_ref = bf16[2,32,1024]{2,1,0:T(8,128)(2,1)} custom-call(bf16[32,1024]{1,0:T(8,128)(2,1)} %copy_bitcast_fusion.x_ref), custom_call_target="tpu_custom_call" | custom-call | tf_op jit(solution)/shard_map/pallas_call | solution.py:69
  112.4 10.0 %shard_map.152.x_ref = bf16[4,2,32,1024]{3,2,1,0:T(8,128)(2,1)} custom-call(bf16[2,32,1024]{2,1,0:T(8,128)(2,1)} %shard_map.151.x_ref), custom_call_target="tpu_custom_call" | custom-call | tf_op jit(solution)/shard_map/pallas_call | solution.py:69
  122.5 9.3 %shard_map.153 = bf16[2,4,2,32,1024]{4,3,2,1,0:T(8,128)(2,1)} custom-call(bf16[4,2,32,1024]{3,2,1,0:T(8,128)(2,1)} %shard_map.152.x_ref), custom_call_target="tpu_custom_call" | custom-call | tf_op jit(solution)/shard_map/pallas_call | solution.py:69
  134.7 6.2 %shard_map.154 = bf16[4,32,128]{2,1,0:T(8,128)(2,1)} custom-call(bf16[4,32,128]{2,1,0:T(8,128)(2,1)} %reshape.286.x_ref), custom_call_target="tpu_custom_call" | custom-call | tf_op jit(solution)/shard_map/pallas_call | solution.py:69
  142.3 41.9 %shard_map.155 = bf16[8,128,640]{2,1,0:T(8,128)(2,1)} custom-call(bf16[128,640]{1,0:T(8,128)(2,1)} %copy-done.5), custom_call_target="tpu_custom_call" | custom-call | tf_op jit(solution)/shard_map/pallas_call | solution.py:157
  184.2 2.6 convolution_convert_fusion.2
  193.6 9.3 %shard_map.156 = bf16[4,256,256]{2,1,0:T(8,128)(2,1)} custom-call(bf16[4,256,256]{2,1,0:T(8,128)(2,1)} %fusion.17.x_ref), custom_call_target="tpu_custom_call" | custom-call | tf_op jit(solution)/shard_map/pallas_call | solution.py:69
  205.2 24.4 %shard_map.157 = bf16[8,256,128]{2,1,0:T(8,128)(2,1)} custom-call(bf16[256,128]{1,0:T(8,128)(2,1)} %slice.82.x_ref), custom_call_target="tpu_custom_call" | custom-call | tf_op jit(solution)/shard_map/pallas_call | solution.py:157
  234.4 7.6 %shard_map.158 = bf16[4,256,128]{2,1,0:T(8,128)(2,1)} custom-call(bf16[256,128]{1,0:T(8,128)(2,1)} %pad.15.x_ref), custom_call_target="tpu_custom_call" | custom-call | tf_op jit(solution)/shard_map/pallas_call | solution.py:69
  246.3 15.4 %shard_map.159 = bf16[2,4,2,32,1024]{4,3,2,1,0:T(8,128)(2,1)} custom-call(bf16[2,4,2,32,1024]{4,3,2,1,0:T(8,128)(2,1)} %bitcast.97), custom_call_target="tpu_custom_call" | custom-call | tf_op jit(solution)/shard_map/pallas_call | solution.py:69
  261.7 2.4 reduce_sum.164.x_ref
  264.1 11.6 %shard_map.160 = bf16[4,2,32,1024]{3,2,1,0:T(8,128)(2,1)} custom-call(bf16[4,2,32,1024]{3,2,1,0:T(8,128)(2,1)} %reduce_sum.164.x_ref), custom_call_target="tpu_custom_call" | custom-call | tf_op jit(solution)/shard_map/pallas_call | solution.py:69
  277.5 16.3 %shard_map.161 = bf16[2,32,1024]{2,1,0:T(8,128)(2,1)} custom-call(bf16[2,32,1024]{2,1,0:T(8,128)(2,1)} %reduce_sum.165.x_ref), custom_call_target="tpu_custom_call" | custom-call | tf_op jit(solution)/shard_map/pallas_call | solution.py:69
  295.4 15.3 %shard_map.162.x_ref = bf16[2,32,1024]{2,1,0:T(8,128)(2,1)} custom-call(bf16[32,1024]{1,0:T(8,128)(2,1)} %add_convert_fusion.1.x_ref), custom_call_target="tpu_custom_call" | custom-call | tf_op jit(solution)/shard_map/pallas_call | solution.py:69
  310.7 11.0 %shard_map.163.x_ref = bf16[4,2,32,1024]{3,2,1,0:T(8,128)(2,1)} custom-call(bf16[2,32,1024]{2,1,0:T(8,128)(2,1)} %shard_map.162.x_ref), custom_call_target="tpu_custom_call" | custom-call | tf_op jit(solution)/shard_map/pallas_call | solution.py:69
  321.7 6.0 %shard_map.164 = bf16[2,4,2,32,1024]{4,3,2,1,0:T(8,128)(2,1)} custom-call(bf16[4,2,32,1024]{3,2,1,0:T(8,128)(2,1)} %shard_map.163.x_ref), custom_call_target="tpu_custom_call" | custom-call | tf_op jit(solution)/shard_map/pallas_call | solution.py:69
  335.4 10.1 %shard_map.165 = bf16[4,384,128]{2,1,0:T(8,128)(2,1)} custom-call(bf16[4,384,128]{2,1,0:T(8,128)(2,1)} %fusion.22.x_ref), custom_call_target="tpu_custom_call" | custom-call | tf_op jit(solution)/shard_map/pallas_call | solution.py:69
  351.8 6.8 %shard_map.166 = bf16[4,64,128]{2,1,0:T(8,128)(2,1)} custom-call(bf16[4,64,128]{2,1,0:T(8,128)(2,1)} %bitcast.124), custom_call_target="tpu_custom_call" | custom-call | tf_op jit(solution)/shard_map/pallas_call | solution.py:69
  362.7 2.3 copy.99
  365.0 6.5 %shard_map.167 = bf16[2,4,2,128,256]{4,3,2,1,0:T(8,128)(2,1)} custom-call(bf16[2,4,2,128,256]{4,3,2,1,0:T(8,128)(2,1)} %bitcast.99), custom_call_target="tpu_custom_call" | custom-call | tf_op jit(solution)/shard_map/pallas_call | solution.py:69
  371.5 2.3 reduce_sum.170.x_ref
  373.9 11.6 %shard_map.168 = bf16[4,2,128,256]{3,2,1,0:T(8,128)(2,1)} custom-call(bf16[4,2,128,256]{3,2,1,0:T(8,128)(2,1)} %reduce_sum.170.x_ref), custom_call_target="tpu_custom_call" | custom-call | tf_op jit(solution)/shard_map/pallas_call | solution.py:69
  387.3 14.1 %shard_map.169 = bf16[2,128,256]{2,1,0:T(8,128)(2,1)} custom-call(bf16[2,128,256]{2,1,0:T(8,128)(2,1)} %reduce_sum.171.x_ref), custom_call_target="tpu_custom_call" | custom-call | tf_op jit(solution)/shard_map/pallas_call | solution.py:69
  (132 shorter events, 55.6 us)
Async XLA Ops:
  0.0 25.6 %copy-start = (bf16[8192,128]{1,0:T(8,128)(2,1)S(1)}, bf16[8192,128]{1,0:T(8,128)(2,1)}, u32[]{:S(2)}) copy-start(bf16[8192,128]{1,0:T(8,128)(2,1)} %param.19) | copy-start | bytes 6291460
  25.6 12.3 %copy-start.6 = (s32[8,4,128]{2,1,0:T(4,128)S(1)}, s32[8,4,128]{2,1,0:T(4,128)}, u32[]{:S(2)}) copy-start(s32[8,4,128]{2,1,0:T(4,128)} %shard_map.146) | copy-start | bytes 49156
  112.4 20.9 %copy-start.7 = (bf16[128,128]{1,0:T(8,128)(2,1)S(1)}, bf16[128,128]{1,0:T(8,128)(2,1)}, u32[]{:S(2)}) copy-start(bf16[128,128]{1,0:T(8,128)(2,1)} %param.21) | copy-start | bytes 98308
  112.4 20.9 %copy-start.8 = (bf16[128,128]{1,0:T(8,128)(2,1)S(1)}, bf16[128,128]{1,0:T(8,128)(2,1)}, u32[]{:S(2)}) copy-start(bf16[128,128]{1,0:T(8,128)(2,1)} %param.22) | copy-start | bytes 98308
  112.4 21.0 %copy-start.9 = (bf16[128,128]{1,0:T(8,128)(2,1)S(1)}, bf16[128,128]{1,0:T(8,128)(2,1)}, u32[]{:S(2)}) copy-start(bf16[128,128]{1,0:T(8,128)(2,1)} %param.23) | copy-start | bytes 98308
  122.5 10.9 %copy-start.10 = (bf16[128,128]{1,0:T(8,128)(2,1)S(1)}, bf16[128,128]{1,0:T(8,128)(2,1)}, u32[]{:S(2)}) copy-start(bf16[128,128]{1,0:T(8,128)(2,1)} %param.26) | copy-start | bytes 98308
  122.5 10.9 %copy-start.11 = (bf16[2,32,128]{2,1,0:T(8,128)(2,1)S(1)}, bf16[2,32,128]{2,1,0:T(8,128)(2,1)}, u32[]{:S(2)}) copy-start(bf16[2,32,128]{2,1,0:T(8,128)(2,1)} %param.27) | copy-start | bytes 49156
  122.5 11.1 %copy-start.12 = (bf16[2,32,128]{2,1,0:T(8,128)(2,1)S(1)}, bf16[2,32,128]{2,1,0:T(8,128)(2,1)}, u32[]{:S(2)}) copy-start(bf16[2,32,128]{2,1,0:T(8,128)(2,1)} %param.28) | copy-start | bytes 49156
  141.6 0.7 copy-start.5
  186.8 4.2 %copy-start.2 = (bf16[2,4,2,32,1024]{4,3,2,1,0:T(8,128)(2,1)S(1)}, bf16[2,4,2,32,1024]{4,3,2,1,0:T(8,128)(2,1)}, u32[]{:S(2)}) copy-start(bf16[2,4,2,32,1024]{4,3,2,1,0:T(8,128)(2,1)} %shard_map.153) | copy-start | bytes 3145732
  191.6 38.0 %copy-start.13 = (s32[2]{0:T(128)S(1)}, s32[2]{0:T(128)}, u32[]{:S(2)}) copy-start(s32[2]{0:T(128)} %param.17) | copy-start | bytes 28
  230.9 2.3 copy-start.3
  261.7 33.0 %copy-start.4 = (bf16[8,32,128]{2,1,0:T(8,128)(2,1)S(1)}, bf16[8,32,128]{2,1,0:T(8,128)(2,1)}, u32[]{:S(2)}) copy-start(bf16[8,32,128]{2,1,0:T(8,128)(2,1)} %shard_map.150) | copy-start | bytes 196612
  327.7 3.3 copy-start.1
  333.8 12.9 %copy-start.14 = (s32[2]{0:T(128)S(1)}, s32[2]{0:T(128)}, u32[]{:S(2)}) copy-start(s32[2]{0:T(128)} %param.18) | copy-start | bytes 28
  371.5 30.8 %slice-start = ((bf16[4,384,128]{2,1,0:T(8,128)(2,1)}), bf16[4,128,128]{2,1,0:T(8,128)(2,1)S(1)}, s32[]{:S(2)}) async-start(bf16[4,384,128]{2,1,0:T(8,128)(2,1)} %shard_map.165), calls=%async_computation | async-start | bytes 262144 | tf_op jit(solution)/shard_map/slice | solution.py:303

commit v2 on v1

--- a/solution.py
+++ b/solution.py
@@ -168,16 +168,136 @@
     return jnp.sum(blocks.astype(F32), axis=0)
 
 
-def scatter_sum(x, ident):
-    x = fold(push(x, LINE_CORE, ident, False)).astype(BF16)
-    x = fold(push(x, LINE_X, ident + 1, False)).astype(BF16)
-    return fold(push(x, LINE_ZH, ident + 2, False))
-
-
-def spread(x, ident):
-    x = push(x, LINE_ZH, ident, True)
-    x = push(x, LINE_X, ident + 1, True)
-    return push(x, LINE_CORE, ident + 2, True)
+def vocab_kernel(mode, *refs):
+    if mode == "rows":
+        x_ref, own_ref, all_ref = refs[:3]
+        refs = refs[3:]
+    elif mode == "terms":
+        x_ref, base_ref, all_ref = refs[:3]
+        refs = refs[3:]
+    else:
+        x_ref, own_ref = refs[:2]
+        refs = refs[2:]
+    got_core, part, got_x, half, got_zh, piece = refs[:6]
+    core_s, core_r, x_s, x_r, zh_s, zh_r, z_s, z_r, x2_s, x2_r, core2_s, core2_r, local = refs[6:]
+    core, place, z, zh = place_on(LINE_CORE), place_on(LINE_X), place_on(LINE_Z), place_on(LINE_ZH)
+    lines = [LINE_CORE, LINE_X, LINE_ZH] + ([LINE_Z] if mode == "rows" else [])
+    barrier = pltpu.get_barrier_semaphore()
+    met = 0
+    for line in lines:
+        for shift in range(1, line[1]):
+            target, _ = peer_of(line, shift)
+            pl.semaphore_signal(barrier, inc=1, device_id=target, device_id_type=MESH)
+            met += 1
+    pl.semaphore_wait(barrier, met)
+
+    def send(source, target_ref, line, shift, send_sem, recv_sem):
+        copy = pltpu.make_async_remote_copy(
+            src_ref=source,
+            dst_ref=target_ref,
+            send_sem=send_sem,
+            recv_sem=recv_sem,
+            device_id=peer_of(line, shift)[0],
+            device_id_type=MESH,
+        )
+        copy.start()
+        return copy
+
+    core_copies = []
+    for shift in (1, 2, 3, 0):
+        other = lax.rem(place + shift, 4)
+        core_copies.append(
+            send(x_ref.at[1 - core, other], got_core.at[other], LINE_CORE, 1, core_s.at[shift], core_r.at[shift])
+        )
+    x_copies = []
+    for order, shift in enumerate((1, 2, 3, 0)):
+        other = lax.rem(place + shift, 4)
+        core_copies[order].wait()
+        part[other] = (x_ref[core, other].astype(F32) + got_core[other].astype(F32)).astype(BF16)
+        if shift:
+            x_copies.append(
+                send(part.at[other], got_x.at[shift - 1], LINE_X, shift, x_s.at[shift - 1], x_r.at[shift - 1])
+            )
+    total = part[place].astype(F32)
+    for shift in range(1, 4):
+        x_copies[shift - 1].wait()
+        total = total + got_x[shift - 1].astype(F32)
+    half[...] = total.astype(BF16)
+    if mode == "final":
+        send(half.at[1 - zh], got_zh, LINE_ZH, 1, zh_s, zh_r).wait()
+        own_ref[...] = half[zh].astype(F32) + got_zh[...].astype(F32)
+        return
+    send(half, got_zh, LINE_ZH, 1, zh_s, zh_r).wait()
+    total = half[...].astype(F32) + got_zh[...].astype(F32)
+    if mode == "rows":
+        piece[...] = total.astype(BF16)
+        cols = piece.shape[2]
+        mine = pl.ds(pl.multiple_of(z * cols, cols), cols)
+        z_copies = []
+        for shift in range(1, LINE_Z[1]):
+            _, other = peer_of(LINE_Z, shift)
+            z_copies.append(
+                send(piece.at[other], own_ref.at[:, mine], LINE_Z, shift, z_s.at[shift - 1], z_r.at[shift - 1])
+            )
+        own_ref[:, mine] = piece[z]
+        for copy in z_copies:
+            copy.wait()
+        block = own_ref
+    else:
+        piece[...] = (base_ref[...].astype(F32) + total).astype(BF16)
+        block = piece
+    keep = pltpu.make_async_copy(block, all_ref.at[core, place], local)
+    keep.start()
+    copies = [send(block, all_ref.at[core, place], LINE_CORE, 1, core2_s.at[0], core2_r.at[0])]
+    x_copies = []
+    for shift in range(1, 4):
+        x_copies.append(
+            send(block, all_ref.at[core, place], LINE_X, shift, x2_s.at[shift - 1], x2_r.at[shift - 1])
+        )
+    for shift in range(1, 4):
+        x_copies[shift - 1].wait()
+        source = lax.rem(place + 4 - shift, 4)
+        copies.append(
+            send(all_ref.at[core, source], all_ref.at[core, source], LINE_CORE, 1, core2_s.at[shift], core2_r.at[shift])
+        )
+    for copy in copies:
+        copy.wait()
+    keep.wait()
+
+
+def vocab_call(mode, ident, x, base=None):
+    block = x.shape[2:]
+    vmem = pl.BlockSpec(memory_space=pltpu.VMEM)
+    if mode == "rows":
+        own = (block[1], block[0] * block[2])
+        out = (jax.ShapeDtypeStruct(own, BF16), jax.ShapeDtypeStruct((2, 4) + own, BF16))
+    elif mode == "terms":
+        out = jax.ShapeDtypeStruct(x.shape, BF16)
+    else:
+        out = jax.ShapeDtypeStruct(block[1:], F32)
+    operands = (x,) if base is None else (x, base)
+    crossing = block[1:] if mode == "final" else block
+
+    def sems(count):
+        return [pltpu.SemaphoreType.DMA((count,))] * 2
+
+    single = pltpu.SemaphoreType.DMA
+    return pl.pallas_call(
+        functools.partial(vocab_kernel, mode),
+        out_shape=out,
+        in_specs=[vmem] * len(operands),
+        out_specs=(vmem, vmem) if mode == "rows" else vmem,
+        scratch_shapes=[
+            pltpu.VMEM((4,) + block, BF16),
+            pltpu.VMEM((4,) + block, BF16),
+            pltpu.VMEM((3,) + block, BF16),
+            pltpu.VMEM(block, BF16),
+            pltpu.VMEM(crossing, BF16),
+            pltpu.VMEM(block, BF16),
+        ]
+        + sems(4) + sems(3) + [single, single] + sems(7) + sems(3) + sems(4) + [single],
+        compiler_params=pltpu.CompilerParams(collective_id=ident, has_side_effects=True),
+    )(*operands)
 
 
 def split_sum(values):
@@ -223,13 +343,14 @@
     heads = 2
     row = n_y * tokens
     row_tokens = pairs * row
-    piece = row_tokens // n_v
+    pieces = n_v // LINE_ZH[1]
+    piece = row_tokens // pieces
 
     ids = jnp.where(keep_mask != 0, token_ids, -1).reshape(1, pairs * tokens)
     ids = push(ids, LINE_Y, 0, True)
     ids = push(ids.reshape(n_y, pairs * tokens), LINE_Z, 1, True)
     ids = ids.reshape(n_z, n_y, pairs, tokens).transpose(0, 2, 1, 3)
-    ids = ids.reshape(n_z, n_v, piece).transpose(1, 0, 2).reshape(-1)
+    ids = ids.reshape(n_z, pieces, piece).transpose(1, 0, 2).reshape(-1)
 
     pos = cross_keys.shape[1]
     both = jnp.stack(
@@ -238,7 +359,8 @@
     both = both.transpose(0, 2, 1, 3, 4).reshape(n_y, pos, 2 * DH)
     both = push(both, LINE_Y, 2, False).reshape(n_y * pos, 2 * DH)
     weights = jnp.concatenate([query_weight, key_weight, value_weight, cross_query_weight, both], axis=1)
-    weights = relay(weights, LINE_Z, 3)
+    same_y = [[z * n_y + y for z in range(n_z)] for y in range(n_y)]
+    weights = lax.all_gather(weights, "seq", axis_index_groups=same_y)
     head_cols = query_weight.shape[1]
     weights = weights.reshape(n_z * cols, 4 * head_cols + 2 * DH)
     source_both = weights[:, 4 * head_cols :]
@@ -248,10 +370,8 @@
     inside = (local_ids >= 0) & (local_ids < shard_rows)
     picked = jnp.take(embed_table, jnp.clip(local_ids, 0, shard_rows - 1), axis=0)
     picked = jnp.where(inside[:, None], picked, jnp.zeros_like(picked))
-    own_rows = scatter_sum(picked.reshape(2, 4, 2, n_z * piece, cols), 4).astype(BF16)
-    own_rows = push(own_rows.reshape(n_z, piece, cols), LINE_Z, 7, False)
-    own_rows = own_rows.transpose(1, 0, 2).reshape(piece, quarter)
-    embedded = spread(own_rows, 8).reshape(row_tokens, quarter)
+    own_rows, embedded = vocab_call("rows", 4, picked.reshape(2, 4, n_z, piece, cols))
+    embedded = embedded.reshape(row_tokens, quarter)
 
     def part_of_gain(gain):
         return lax.dynamic_index_in_dim(gain.reshape(n_z, n_y, cols), y_index, 1, False).reshape(quarter)
@@ -282,8 +402,8 @@
     context = context.reshape(pairs, heads, row, DH).transpose(0, 2, 1, 3).reshape(row_tokens, heads * DH)
     out_part = lax.dynamic_index_in_dim(self_out_weight.reshape(-1, n_z, n_y, cols), y_index, 2, False)
     terms = jnp.dot(context, out_part.reshape(-1, quarter), preferred_element_type=F32).astype(BF16)
-    after = own_rows.astype(F32) + scatter_sum(terms.reshape(2, 4, 2, piece, quarter), 14)
-    after = spread(after.astype(BF16), 17).reshape(row_tokens, quarter)
+    after = vocab_call("terms", 5, terms.reshape(2, 4, piece, quarter), own_rows)
+    after = after.reshape(row_tokens, quarter)
 
     wide = after.astype(F32)
     squares = jnp.sum(wide * wide, axis=-1)
@@ -313,7 +433,7 @@
     terms = jnp.dot(context, cross_out_weight, preferred_element_type=F32).astype(BF16)
     share = width // n_v
     terms = terms.reshape(pairs * tokens, 2, 4, 2, share).transpose(3, 2, 1, 0, 4)
-    result = residual.astype(F32) + scatter_sum(terms, 22)
+    result = residual.astype(F32) + vocab_call("final", 6, terms)
     return result.astype(BF16).reshape(pairs, tokens, share)
 
 

time: 406 us -> 311 us (0.77)
  Pallas kernels: 320 us -> 226 us
  other arithmetic: 32.8 us -> 19.6 us
  between operations: 0.86 us -> 13.9 us
    pallas_call x23 -> x7, Pallas kernels: 254 us -> 64.6 us  [push(): pl.pallas_call(functools.partial(push_kernel, line, gather), out_shape=ja...]
    pallas_call x0 -> x3, Pallas kernels: none -> 139 us  [vocab_call(): pl.pallas_call(functools.partial(vocab_kernel, mode), out_shape=out, in_s...]
    pallas_call x2 -> x1, Pallas kernels: 66.2 us -> 23.3 us  [relay(): pl.pallas_call(functools.partial(relay_kernel, line), out_shape=jax.Shape...]
    reduce_sum x11 -> x2, other arithmetic: 18.1 us -> 2.14 us  [fold(): return jnp.sum(blocks.astype(F32), axis=0)]
  transfers between devices with their start and end apart: 0 -> 1, of which waited for: 0 -> 0; matrix products, arithmetic and copies ran while one was open for 0% -> 9% of each run, Pallas kernels for 0% -> 27%
where the time goes in v2:
time: 311 us; the launch traced here: 309 us
  Pallas kernels  226 us (73%)
  local copies, waits for them, and re-layouts  36.9 us (12%)
  other arithmetic  19.6 us (6%)
  between operations  13.9 us (4%)
  matrix products  11.9 us (4%)
    pallas_call x3, Pallas kernels, vocab_call(): pl.pallas_call(functools.partial(vocab_kernel, mode), out_shape=out, in_s...  139 us
    pallas_call x7, Pallas kernels, push(): pl.pallas_call(functools.partial(push_kernel, line, gather), out_shape=ja...  64.6 us
    pallas_call x1, Pallas kernels, relay(): pl.pallas_call(functools.partial(relay_kernel, line), out_shape=jax.Shape...  23.3 us
    gather x1, local copies, waits for them, and re-layouts, on_device(): jnp.take(embed_table, jnp.clip(local_ids, 0, shard_rows - 1), axis=0)  12.1 us
    unnamed x26, local copies, waits for them, and re-layouts  6.73 us
  transfers between devices with their start and end apart: 1, of which 0 were waited for; matrix products, arithmetic and copies ran while one was open for 9% of the time, Pallas kernels for 27%

profile of v2, /device:TPU:1, one launch (start us, length us, event | category | flops | bytes accessed | tf_op | source)
XLA Modules:
  0.0 308.7 jit_solution(15682733790689669636)
XLA Ops:
  10.1 8.0 %shard_map.148 = bf16[4,32,128]{2,1,0:T(8,128)(2,1)} custom-call(bf16[4,32,128]{2,1,0:T(8,128)(2,1)} %reshape.278.x_ref), custom_call_target="tpu_custom_call" | custom-call | tf_op jit(solution)/shard_map/pallas_call | solution.py:69
  23.2 5.9 %shard_map.145 = s32[4,1,128]{2,1,0:T(1,128)} custom-call(s32[1,128]{1,0:T(1,128)} %reshape.274.x_ref), custom_call_target="tpu_custom_call" | custom-call | tf_op jit(solution)/shard_map/pallas_call | solution.py:69
  29.1 14.4 %shard_map.146 = s32[8,4,128]{2,1,0:T(4,128)} custom-call(s32[4,128]{1,0:T(4,128)} %bitcast.134), custom_call_target="tpu_custom_call" | custom-call | tf_op jit(solution)/shard_map/pallas_call | solution.py:69
  45.4 12.1 %gather_fusion = bf16[4096,128]{1,0:T(8,128)(2,1)S(1)} fusion(bf16[8192,128]{1,0:T(8,128)(2,1)S(1)} %copy-done, s32[4096]{0:T(1024)S(1)} %broadcast_clamp_fusion), kind=kCustom, calls=%fused_computation | custom fusion | bytes 2113536 | tf_op jit(solution)/shard_map/jit(_take)/gather | solution.py:371
  57.5 2.5 select_select_fusion.refs_0_
  60.0 61.9 %shard_map.147 = (bf16[64,1024]{1,0:T(8,128)(2,1)}, bf16[2,4,64,1024]{3,2,1,0:T(8,128)(2,1)}) custom-call(bf16[2,4,8,64,128]{4,3,2,1,0:T(8,128)(2,1)} %select_select_fusion.refs_0_), custom_call_target="tpu_custom_call" | custom-call | tf_op jit(solution)/shard_map/pallas_call | solution.py:285
  122.0 1.6 multiply_reduce_fusion.1
  124.5 2.3 copy.78
  131.5 1.2 fusion.1
  132.7 2.2 convolution_convert_fusion.2
  136.4 1.0 fusion.17.x_ref
  137.4 11.8 %shard_map.149 = bf16[4,256,256]{2,1,0:T(8,128)(2,1)} custom-call(bf16[4,256,256]{2,1,0:T(8,128)(2,1)} %fusion.17.x_ref), custom_call_target="tpu_custom_call" | custom-call | tf_op jit(solution)/shard_map/pallas_call | solution.py:69
  149.3 1.1 convert_reduce_fusion
  151.5 23.3 %shard_map.150 = bf16[8,256,128]{2,1,0:T(8,128)(2,1)} custom-call(bf16[256,128]{1,0:T(8,128)(2,1)} %slice.82.x_ref), custom_call_target="tpu_custom_call" | custom-call | tf_op jit(solution)/shard_map/pallas_call | solution.py:157
  174.8 1.8 fusion.40
  178.4 7.6 %shard_map.151 = bf16[4,256,128]{2,1,0:T(8,128)(2,1)} custom-call(bf16[256,128]{1,0:T(8,128)(2,1)} %pad.15.x_ref), custom_call_target="tpu_custom_call" | custom-call | tf_op jit(solution)/shard_map/pallas_call | solution.py:69
  186.0 1.1 copy.77
  187.1 1.5 convolution_convert_fusion.1
  188.6 49.0 %shard_map.152 = bf16[2,4,64,1024]{3,2,1,0:T(8,128)(2,1)} custom-call(bf16[2,4,64,1024]{3,2,1,0:T(8,128)(2,1)} %bitcast.103, bf16[64,1024]{1,0:T(8,128)(2,1)} %get-tuple-element.8.refs_1_), custom_call_target="tpu_custom_call" | custom-call | tf_op jit(solution)/shard_map/pallas_call | solution.py:285
  237.6 1.5 multiply_reduce_fusion
  239.1 1.6 fusion
  240.7 1.4 convolution_convert_fusion.3
  244.3 10.3 %shard_map.153 = bf16[4,384,128]{2,1,0:T(8,128)(2,1)} custom-call(bf16[4,384,128]{2,1,0:T(8,128)(2,1)} %fusion.22.x_ref), custom_call_target="tpu_custom_call" | custom-call | tf_op jit(solution)/shard_map/pallas_call | solution.py:69
  254.6 1.0 convert_reduce_fusion.1
  255.8 1.4 fusion.41
  257.5 1.4 fusion.6
  259.7 6.5 %shard_map.154 = bf16[4,64,128]{2,1,0:T(8,128)(2,1)} custom-call(bf16[4,64,128]{2,1,0:T(8,128)(2,1)} %bitcast.124), custom_call_target="tpu_custom_call" | custom-call | tf_op jit(solution)/shard_map/pallas_call | solution.py:69
  267.2 1.6 convolution_convert_fusion
  268.9 1.3 copy.87
  270.2 2.3 copy.88
  272.5 27.6 %shard_map.155 = f32[128,256]{1,0:T(8,128)} custom-call(bf16[2,4,2,128,256]{4,3,2,1,0:T(8,128)(2,1)} %bitcast.105), custom_call_target="tpu_custom_call" | custom-call | tf_op jit(solution)/shard_map/pallas_call | solution.py:285
  300.3 1.6 fusion.27
  (89 shorter events, 24.9 us)
Async XLA Ops:
  6.5 38.8 %copy-start = (bf16[8192,128]{1,0:T(8,128)(2,1)S(1)}, bf16[8192,128]{1,0:T(8,128)(2,1)}, u32[]{:S(2)}) copy-start(bf16[8192,128]{1,0:T(8,128)(2,1)} %param.19) | copy-start | bytes 6291460
  6.5 126.2 %all-gather.3.cloned.1.call-start = ((), (), s32[]{:S(2)}) async-start(), calls=%async_computation | async-start | bytes 1474560 | tf_op jit(solution)/shard_map/all_gather | solution.py:363
  21.1 0.7 copy-start.4
  60.0 66.7 %copy-start.5 = (s32[2]{0:T(128)S(1)}, s32[2]{0:T(128)}, u32[]{:S(2)}) copy-start(s32[2]{0:T(128)} %param.17) | copy-start | bytes 28
  60.0 67.3 %copy-start.6 = (s32[2]{0:T(128)S(1)}, s32[2]{0:T(128)}, u32[]{:S(2)}) copy-start(s32[2]{0:T(128)} %param.18) | copy-start | bytes 28
  121.9 9.5 %copy-start.2 = (bf16[2,4,64,1024]{3,2,1,0:T(8,128)(2,1)S(1)}, bf16[2,4,64,1024]{3,2,1,0:T(8,128)(2,1)}, u32[]{:S(2)}) copy-start(bf16[2,4,64,1024]{3,2,1,0:T(8,128)(2,1)} %get-tuple-element.7) | copy-start | bytes 3145732
  136.4 38.4 %copy-start.7 = (s32[256]{0:T(256)S(1)}, s32[256]{0:T(256)}, u32[]{:S(2)}) copy-start(s32[256]{0:T(256)} %iota_add_fusion) | copy-start | bytes 3076
  174.8 2.3 copy-start.3
  239.1 3.3 %copy-start.1 = (bf16[2,4,64,1024]{3,2,1,0:T(8,128)(2,1)S(1)}, bf16[2,4,64,1024]{3,2,1,0:T(8,128)(2,1)}, u32[]{:S(2)}) copy-start(bf16[2,4,64,1024]{3,2,1,0:T(8,128)(2,1)} %shard_map.152) | copy-start | bytes 3145732
  270.2 30.0 %slice-start = ((bf16[4,384,128]{2,1,0:T(8,128)(2,1)}), bf16[4,128,128]{2,1,0:T(8,128)(2,1)S(1)}, s32[]{:S(2)}) async-start(bf16[4,384,128]{2,1,0:T(8,128)(2,1)} %shard_map.153), calls=%async_computation.1 | async-start | bytes 262144 | tf_op jit(solution)/shard_map/slice | solution.py:423
Sparse Core Ops, SparseCore 0:
  22.0 66.2 all-gather.2

commit v3 on v0

v3 whole, which is shorter than its diff:
```python
import functools

import jax
import jax.numpy as jnp
from jax import lax
from jax.experimental import pallas as pl
from jax.experimental.pallas import tpu as pltpu
from jax.sharding import PartitionSpec as P

DH = 64
MESH = pl.DeviceIdType.MESH
F32 = jnp.float32
BF16 = jnp.bfloat16

LINE_Y = ("seq", 4, 1)
LINE_Z = ("seq", 8, 4)
LINE_CORE = ("vocab", 2, 1)
LINE_X = ("vocab", 4, 2)
LINE_ZH = ("vocab", 2, 8)


def place_on(line):
    axis, members, stride = line
    return lax.rem(lax.axis_index(axis) // stride, members)


def peer_of(line, shift):
    axis, members, stride = line
    here = lax.axis_index(axis)
    mine = lax.rem(here // stride, members)
    other = lax.rem(mine + shift, members)
    there = here + (other - mine) * stride
    if axis == "seq":
        return (lax.axis_index("vocab"), there), other
    return (there, lax.axis_index("seq")), other


def greet(devices):
    barrier = pltpu.get_barrier_semaphore()
    for target in devices:
        pl.semaphore_signal(barrier, inc=1, device_id=target, device_id_type=MESH)
    return barrier


def peers_on(line):
    return [peer_of(line, shift)[0] for shift in range(1, line[1])]


def send(source, target_ref, target, send_sem, recv_sem):
    copy = pltpu.make_async_remote_copy(
        src_ref=source,
        dst_ref=target_ref,
        send_sem=send_sem,
        recv_sem=recv_sem,
        device_id=target,
        device_id_type=MESH,
    )
    copy.start()
    return copy


def start_kernel(ids_ref, both_ref, all_ids, both_out, row_ids, own, y_s, y_r, z_s, z_r, b_s, b_r):
    y, z = place_on(LINE_Y), place_on(LINE_Z)
    near, far = peers_on(LINE_Y), peers_on(LINE_Z)
    barrier = greet(near + far)
    keep = [
        pltpu.make_async_copy(ids_ref, row_ids.at[y], own.at[0]),
        pltpu.make_async_copy(both_ref.at[y], both_out.at[y], own.at[1]),
    ]
    for copy in keep:
        copy.start()
    pl.semaphore_wait(barrier, len(near + far))
    copies = [send(ids_ref, row_ids.at[y], near[k], y_s.at[k], y_r.at[k]) for k in range(3)]
    later = []
    for k in range(3):
        other = lax.rem(y + k + 1, 4)
        later.append(send(both_ref.at[other], both_out.at[y], near[k], b_s.at[k], b_r.at[k]))
    for copy in keep + copies:
        copy.wait()
    last = pltpu.make_async_copy(row_ids, all_ids.at[z], own.at[2])
    last.start()
    later += [send(row_ids, all_ids.at[z], far[k], z_s.at[k], z_r.at[k]) for k in range(7)]
    for copy in later + [last]:
        copy.wait()


def sems(count):
    return [pltpu.SemaphoreType.DMA((count,))] * 2


def call(kernel, ident, out, scratch, operands, in_specs=None):
    vmem = pl.BlockSpec(memory_space=pltpu.VMEM)
    return pl.pallas_call(
        kernel,
        out_shape=out,
        in_specs=in_specs or [vmem] * len(operands),
        out_specs=(vmem,) * len(out) if isinstance(out, tuple) else vmem,
        scratch_shapes=scratch,
        compiler_params=pltpu.CompilerParams(collective_id=ident, has_side_effects=True),
    )(*operands)


def near_sum(x_ref, got_core, part, got_x, half, core_s, core_r, x_s, x_r):
    core, place = place_on(LINE_CORE), place_on(LINE_X)
    twin, row = peers_on(LINE_CORE)[0], peers_on(LINE_X)
    order = (1, 2, 3, 0)
    core_copies = []
    for k, shift in enumerate(order):
        other = lax.rem(place + shift, 4)
        core_copies.append(send(x_ref.at[1 - core, other], got_core.at[other], twin, core_s.at[k], core_r.at[k]))
    x_copies = []
    for k, shift in enumerate(order):
        other = lax.rem(place + shift, 4)
        core_copies[k].wait()
        part[other] = (x_ref[core, other].astype(F32) + got_core[other].astype(F32)).astype(BF16)
        if shift:
            x_copies.append(send(part.at[other], got_x.at[k], row[k], x_s.at[k], x_r.at[k]))
    total = part[place].astype(F32)
    for k in range(3):
        x_copies[k].wait()
        total = total + got_x[k].astype(F32)
    half[...] = total.astype(BF16)


def near_sum_scratch(block):
    return [
        pltpu.VMEM((4,) + block, BF16),
        pltpu.VMEM((4,) + block, BF16),
        pltpu.VMEM((3,) + block, BF16),
        pltpu.VMEM(block, BF16),
    ] + sems(4) + sems(3)


def spread(block, all_ref, core_s, core_r, x_s, x_r, local):
    core, place = place_on(LINE_CORE), place_on(LINE_X)
    twin, row = peers_on(LINE_CORE)[0], peers_on(LINE_X)
    keep = pltpu.make_async_copy(block, all_ref.at[core, place], local)
    keep.start()
    copies = [send(block, all_ref.at[core, place], twin, core_s.at[0], core_r.at[0])]
    x_copies = [send(block, all_ref.at[core, place], row[k], x_s.at[k], x_r.at[k]) for k in range(3)]
    for k in range(3):
        x_copies[k].wait()
        source = all_ref.at[core, lax.rem(place + 3 - k, 4)]
        copies.append(send(source, source, twin, core_s.at[k + 1], core_r.at[k + 1]))
    for copy in copies:
        copy.wait()
    keep.wait()


def spread_scratch():
    return sems(4) + sems(3) + [pltpu.SemaphoreType.DMA]


def rows_kernel(x_ref, own_ref, all_ref, *refs):
    near, refs = refs[:8], refs[8:]
    got, z_s, z_r, zh_s, zh_r = refs[:5]
    half = near[3]
    z, zh = place_on(LINE_Z), place_on(LINE_ZH)
    v, s = lax.axis_index("vocab"), lax.axis_index("seq")
    level = peers_on(LINE_Z)
    over_v = peer_of(LINE_ZH, 1)[0][0]
    across = [(over_v, peer_of(LINE_Z, k)[0][1]) for k in range(8)]
    devices = peers_on(LINE_CORE) + peers_on(LINE_X) + level + across
    barrier = greet(devices)
    pl.semaphore_wait(barrier, len(devices))
    near_sum(x_ref, *near)
    copies = []
    for k in (4, 3, 5, 2, 6, 1, 7, 0):
        other = lax.rem(z + k, 8)
        copies.append(send(half.at[other], got.at[zh, z], across[k], zh_s.at[k], zh_r.at[k]))
        if k:
            copies.append(send(half.at[other], got.at[zh, z], level[k - 1], z_s.at[k - 1], z_r.at[k - 1]))
    got[zh, z] = half[z]
    for copy in copies:
        copy.wait()
    cols = got.shape[3]
    for k in range(8):
        own_ref[:, k * cols : (k + 1) * cols] = (got[0, k].astype(F32) + got[1, k].astype(F32)).astype(BF16)
    spread(own_ref, all_ref, *refs[5:])


def embed_rows(x, ident):
    block = x.shape[2:]
    own = (block[1], block[0] * block[2])
    out = (jax.ShapeDtypeStruct(own, BF16), jax.ShapeDtypeStruct((2, 4) + own, BF16))
    scratch = near_sum_scratch(block) + [pltpu.VMEM((2,) + block, BF16)] + sems(7) + sems(8) + spread_scratch()
    return call(rows_kernel, ident, out, scratch, (x,))


def lanes_of(shape):
    return lax.broadcasted_iota(jnp.int32, shape, 1)


def with_squares(product, squares, lane):
    high = squares.astype(BF16).astype(F32)
    at = lanes_of(product.shape)
    return jnp.where(at == lane, high, jnp.where(at == lane + 1, squares - high, product))


def scaled_sum(got, rows, lane, width):
    total = got[0, :rows].astype(F32)
    for k in range(1, 4):
        total = total + got[k, :rows].astype(F32)
    squares = total[:, lane : lane + 1] + total[:, lane + 1 : lane + 2]
    return total * lax.rsqrt(squares / width + 1e-06)


def attend(query, both, visible, head):
    scores = lax.dot_general(query, both, (((1,), (1,)), ((), ())), preferred_element_type=F32)
    scores = jnp.where(visible, scores, -jnp.inf)
    raised = jnp.exp(scores - jnp.max(scores, axis=-1, keepdims=True))
    totals = jnp.sum(raised, axis=-1, keepdims=True)
    mixed = jnp.dot(raised.astype(BF16), both, preferred_element_type=F32) / totals
    moved = jnp.where(head == 0, pltpu.roll(mixed, DH, 1), mixed)
    return jnp.where(lanes_of(moved.shape) // DH == head, moved, 0.0).astype(BF16)


def self_kernel(width, length_ref, emb_ref, own_ref, gain_ref, weight_ref, out_ref, all_ref, *refs):
    blocks, got_y, kv, got_ctx, terms, y_s, y_r, up_s, up_r, c_s, c_r, got_zh, piece, zh_s, zh_r = refs[:15]
    near, far = refs[15:23], refs[23:]
    half = near[3]
    y, z = place_on(LINE_Y), place_on(LINE_Z)
    side = peers_on(LINE_Y)
    up, down = peer_of(LINE_Z, 1)[0], peer_of(LINE_Z, 7)[0]
    has_up, has_down = z < 7, z > 0
    devices = peers_on(LINE_CORE) + peers_on(LINE_X) + peers_on(LINE_ZH) + side
    barrier = greet(devices)

    @pl.when(has_up)
    def _():
        pl.semaphore_signal(barrier, inc=1, device_id=up, device_id_type=MESH)

    @pl.when(has_down)
    def _():
        pl.semaphore_signal(barrier, inc=1, device_id=down, device_id_type=MESH)

    row = emb_ref.shape[0] // 2
    for pair in range(2):
        wide = emb_ref[pair * row : (pair + 1) * row].astype(F32)
        squares = jnp.sum(wide * wide, axis=-1, keepdims=True)
        scaled = (wide * gain_ref[...]).astype(BF16)
        for head in range(2):
            weight = weight_ref[:, head * 4 * DH : (head + 1) * 4 * DH]
            product = jnp.dot(scaled, weight, preferred_element_type=F32)
            blocks[2 * pair + head] = with_squares(product, squares, 3 * DH).astype(BF16)
    for k in range(1, 8):

        @pl.when(k > z)
        def _():
            kv[k] = jnp.zeros(kv.shape[1:], BF16)

    @pl.when(has_up & has_down)
    def _():
        pl.semaphore_wait(barrier, len(devices) + 2)

    @pl.when(jnp.logical_not(has_up & has_down))
    def _():
        pl.semaphore_wait(barrier, len(devices) + 1)

    copies = []
    for k in range(3):
        other = lax.rem(y + k + 1, 4)
        copies.append(send(blocks.at[other], got_y.at[y], side[k], y_s.at[k], y_r.at[k]))
    got_y[y] = blocks[y]
    for copy in copies:
        copy.wait()
    qkv = scaled_sum(got_y, row, 3 * DH, width)
    kv[z] = qkv[:, : 2 * DH].astype(BF16)
    query = qkv[:, 2 * DH :]
    query = jnp.where(lanes_of(query.shape) < DH, query, 0.0).astype(BF16)

    chunk = row // 2

    def passing(source, step, part):
        place = kv.at[source, part * chunk : (part + 1) * chunk]
        index = (step - 1) * 2 + part
        return pltpu.make_async_remote_copy(
            src_ref=place,
            dst_ref=place,
            send_sem=up_s.at[index],
            recv_sem=up_r.at[index],
            device_id=up,
            device_id_type=MESH,
        )

    for step in range(1, 9):
        for part in range(2):
            if step > 1:

                @pl.when(z - step + 1 >= 0)
                def _():
                    passing(z - step + 1, step - 1, part).wait_recv()

            if step < 8:

                @pl.when(has_up & (z - step + 1 >= 0))
                def _():
                    passing(z - step + 1, step, part).start()

    pair = y // 2
    both = kv[...].reshape(8 * row, 2 * DH)
    key_pos = lanes_of((row, 8 * row))
    query_pos = z * row + lax.broadcasted_iota(jnp.int32, (row, 8 * row), 0)
    visible = (key_pos <= query_pos) & (key_pos < length_ref[pair])
    got_ctx[y] = attend(query, both, visible, lax.rem(y, 2))
    copies = [send(got_ctx.at[y], got_ctx.at[y], side[k], c_s.at[k], c_r.at[k]) for k in range(3)]
    for step in range(1, 8):
        for part in range(2):

            @pl.when(has_up & (z - step + 1 >= 0))
            def _():
                passing(z - step + 1, step, part).wait_send()

    for copy in copies:
        copy.wait()
    for pair in range(2):
        context = got_ctx[2 * pair] + got_ctx[2 * pair + 1]
        product = jnp.dot(context, out_ref[...], preferred_element_type=F32).astype(BF16)
        terms[pair] = product.reshape(terms.shape[1:])
    near_sum(terms, *near)
    send(half, got_zh, peers_on(LINE_ZH)[0], zh_s.at[0], zh_r.at[0]).wait()
    piece[...] = (own_ref[...].astype(F32) + (half[...].astype(F32) + got_zh[...].astype(F32))).astype(BF16)
    spread(piece, all_ref, *far)


def self_block(ident, width, length, embedded, own_rows, gain, weights, out_weight):
    tokens, quarter = embedded.shape
    row = tokens // 2
    piece = own_rows.shape
    vmem = pl.BlockSpec(memory_space=pltpu.VMEM)
    scratch = (
        [
            pltpu.VMEM((4, row, 4 * DH), BF16),
            pltpu.VMEM((4, row, 4 * DH), BF16),
            pltpu.VMEM((8, row, 2 * DH), BF16),
            pltpu.VMEM((4, row, 2 * DH), BF16),
            pltpu.VMEM((2, 4) + piece, BF16),
        ]
        + sems(3) + sems(14) + sems(3)
        + [pltpu.VMEM(piece, BF16), pltpu.VMEM(piece, BF16)]
        + sems(1) + near_sum_scratch(piece) + spread_scratch()
    )
    operands = (length, embedded, own_rows, gain, weights, out_weight)
    specs = [pl.BlockSpec(memory_space=pltpu.SMEM)] + [vmem] * 5
    out = jax.ShapeDtypeStruct((2, 4) + piece, BF16)
    return call(functools.partial(self_kernel, width), ident, out, scratch, operands, specs)


def cross_kernel(width, length_ref, after_ref, gain_ref, weight_ref, out_ref, result_ref, *refs):
    blocks, got_y, ctx, got_ctx, terms, y_s, y_r, c_s, c_r, got_zh, zh_s, zh_r = refs[:12]
    near = refs[12:]
    half = near[3]
    y, zh = place_on(LINE_Y), place_on(LINE_ZH)
    v = lax.axis_index("vocab")
    side = peers_on(LINE_Y)
    devices = peers_on(LINE_CORE) + peers_on(LINE_X) + peers_on(LINE_ZH) + side
    barrier = greet(devices)
    row = after_ref.shape[0] // 2
    own = row // 4
    cols = 2 * DH
    share = pl.ds(pl.multiple_of((v // 2) * cols, cols), cols)
    for pair in range(2):
        wide = after_ref[pair * row : (pair + 1) * row].astype(F32)
        squares = jnp.sum(wide * wide, axis=-1, keepdims=True)
        scaled = (wide * gain_ref[...]).astype(BF16)
        for head in range(2):
            weight = weight_ref[:, head * 4 * DH + 2 * DH : (head + 1) * 4 * DH]
            product = jnp.dot(scaled, weight, preferred_element_type=F32)
            blocks[2 * pair + head, :row] = with_squares(product, squares, 0).astype(BF16)
        for k in range(4):
            lower = pair * row + k * own
            blocks[k, row + pair * own : row + (pair + 1) * own] = after_ref[lower : lower + own, share]
    pl.semaphore_wait(barrier, len(devices))
    copies = []
    for k in range(3):
        other = lax.rem(y + k + 1, 4)
        copies.append(send(blocks.at[other], got_y.at[y], side[k], y_s.at[k], y_r.at[k]))
    got_y[y] = blocks[y]
    for copy in copies:
        copy.wait()
    query = pltpu.roll(scaled_sum(got_y, row, 0, width), DH, 1)
    query = jnp.where(lanes_of(query.shape) < DH, query, 0.0).astype(BF16)
    both = weight_ref[:, 8 * DH :]
    visible = lanes_of((row, both.shape[0])) < length_ref[y // 2]
    ctx[...] = attend(query, both, visible, lax.rem(y, 2)).reshape(ctx.shape)
    copies = []
    for k in range(3):
        other = lax.rem(y + k + 1, 4)
        copies.append(send(ctx.at[other], got_ctx.at[y], side[k], c_s.at[k], c_r.at[k]))
    got_ctx[y] = ctx[y]
    for copy in copies:
        copy.wait()
    context = jnp.concatenate([got_ctx[0] + got_ctx[1], got_ctx[2] + got_ctx[3]], axis=0)
    out_cols = terms.shape[4]
    for core in range(2):
        for place in range(4):
            for far in range(2):
                lower = (far * 8 + place * 2 + core) * out_cols
                product = jnp.dot(context, out_ref[:, lower : lower + out_cols], preferred_element_type=F32)
                terms[core, place, far] = product.astype(BF16)
    near_sum(terms, *near)
    send(half.at[1 - zh], got_zh, peers_on(LINE_ZH)[0], zh_s.at[0], zh_r.at[0]).wait()
    total = half[zh].astype(F32) + got_zh[...].astype(F32)
    first = 2 * lax.rem(v, 2)
    for k in range(2):
        residual = got_y[first + k, row:].astype(F32)
        lanes = slice(k * cols, (k + 1) * cols)
        result_ref[:, lanes] = (residual + total[:, lanes]).astype(BF16)


def cross_block(ident, width, length, after, gain, weights, out_weight):
    row = after.shape[0] // 2
    own = row // 4
    block = (2, 2 * own, width // 16)
    vmem = pl.BlockSpec(memory_space=pltpu.VMEM)
    scratch = (
        [
            pltpu.VMEM((4, row + 2 * own, 2 * DH), BF16),
            pltpu.VMEM((4, row + 2 * own, 2 * DH), BF16),
            pltpu.VMEM((4, own, 2 * DH), BF16),
            pltpu.VMEM((4, own, 2 * DH), BF16),
            pltpu.VMEM((2, 4) + block, BF16),
        ]
        + sems(3) + sems(3) + [pltpu.VMEM(block[1:], BF16)] + sems(1) + near_sum_scratch(block)
    )
    operands = (length, after, gain, weights, out_weight)
    specs = [pl.BlockSpec(memory_space=pltpu.SMEM)] + [vmem] * 4
    out = jax.ShapeDtypeStruct(block[1:], BF16)
    return call(functools.partial(cross_kernel, width), ident, out, scratch, operands, specs)


def on_device(
    token_ids,
    keep_mask,
    target_length,
    source_length,
    embed_table,
    self_gain,
    query_weight,
    key_weight,
    value_weight,
    self_out_weight,
    cross_gain,
    cross_query_weight,
    cross_keys,
    cross_values,
    cross_out_weight,
):
    pairs, tokens = token_ids.shape
    vocab_index = lax.axis_index("vocab")
    y_index = place_on(LINE_Y)
    n_y, n_z = LINE_Y[1], LINE_Z[1]
    width = self_gain.shape[0]
    quarter = width // n_y
    cols = embed_table.shape[1]
    heads = 2
    row_tokens = pairs * n_y * tokens
    pieces = 8
    piece = row_tokens // pieces

    ids = jnp.where(keep_mask != 0, token_ids, -1).reshape(1, pairs * tokens)
    pos = cross_keys.shape[1]
    both = jnp.stack(
        [cross_keys.reshape(pairs, pos, heads, DH), cross_values.reshape(pairs, pos, heads, DH)], axis=3
    )
    both = both.transpose(0, 2, 1, 3, 4).reshape(n_y, pos, 2 * DH)
    out = (
        jax.ShapeDtypeStruct((n_z, n_y) + ids.shape, ids.dtype),
        jax.ShapeDtypeStruct(both.shape, BF16),
    )
    scratch = [pltpu.VMEM((n_y,) + ids.shape, ids.dtype), pltpu.SemaphoreType.DMA((3,))]
    ids, both = call(start_kernel, 0, out, scratch + sems(3) + sems(7) + sems(3), (ids, both))
    ids = ids.reshape(n_z, n_y, pairs, tokens).transpose(0, 2, 1, 3)
    ids = ids.reshape(n_z, pieces, piece).transpose(1, 0, 2).reshape(-1)

    weights = jnp.stack([key_weight, value_weight, query_weight, cross_query_weight], axis=1)
    weights = weights.reshape(cols, 4, heads, DH).transpose(0, 2, 1, 3).reshape(cols, heads * 4 * DH)
    weights = jnp.concatenate([weights, both.reshape(n_y * pos, 2 * DH)], axis=1)
    same_y = [[z * n_y + y for z in range(n_z)] for y in range(n_y)]
    weights = lax.all_gather(weights, "seq", axis_index_groups=same_y)
    weights = weights.reshape(n_z * cols, weights.shape[2])

    shard_rows = embed_table.shape[0]
    local_ids = ids - vocab_index * shard_rows
    inside = (local_ids >= 0) & (local_ids < shard_rows)
    picked = jnp.take(embed_table, jnp.clip(local_ids, 0, shard_rows - 1), axis=0)
    picked = jnp.where(inside[:, None], picked, jnp.zeros_like(picked))
    own_rows, embedded = embed_rows(picked.reshape(2, 4, n_z, piece, cols), 1)
    embedded = embedded.reshape(row_tokens, quarter)

    def quarter_of(values):
        part = values.reshape(-1, n_z, n_y, cols)
        return lax.dynamic_index_in_dim(part, y_index, 2, False).reshape(-1, quarter)

    out_part = quarter_of(self_out_weight)
    self_part, cross_part = quarter_of(self_gain), quarter_of(cross_gain)
    after = self_block(2, width, target_length, embedded, own_rows, self_part, weights, out_part)
    after = after.reshape(row_tokens, quarter)
    result = cross_block(3, width, source_length, after, cross_part, weights, cross_out_weight)
    return result.reshape(pairs, tokens, result.shape[1])


def solution(mesh):
    return jax.shard_map(
        on_device,
        mesh=mesh,
        in_specs=(
            P(None, "seq"),
            P(None, "seq"),
            P(),
            P(),
            P("vocab", "seq"),
            P(),
            P("seq", "vocab"),
            P("seq", "vocab"),
            P("seq", "vocab"),
            P("vocab", None),
            P(),
            P("seq", "vocab"),
            P(None, "seq", "vocab"),
            P(None, "seq", "vocab"),
            P("vocab", None),
        ),
        out_specs=P(None, "seq", "vocab"),
        check_vma=False,
    )
```

time: 1700 us -> 228 us (0.13)
  waiting for transfers between devices: 1220 us -> 1.63 us
  blocking collectives: 391 us -> 0 us
  Pallas kernels: 0 us -> 181 us
    all_gather x6 -> x1, waiting for transfers between devices: 828 us -> 1.61 us  [on_device(): weights = lax.all_gather(weights, 'seq', axis_index_groups=same_y)]
    all_gather x3 -> x0, blocking collectives: 332 us -> none  [the longest x1 118 us: on_device(): lax.all_gather(cross_values, 'seq', axis=1, tiled=True)]
    psum x2 -> x0, waiting for transfers between devices: 291 us -> none  [the longest x1 256 us: on_device(): lax.psum(arrived.astype(jnp.float32).astype(jnp.bfloat16), 'vocab')]
    pallas_call x0 -> x4, Pallas kernels: none -> 181 us  [call(): pl.pallas_call(kernel, out_shape=out, in_specs=in_specs or [vmem] * len(o...]
    reduce_scatter x1 -> x0, waiting for transfers between devices: 104 us -> none  [on_device(): lax.psum_scatter(cross_terms.astype(jnp.bfloat16), 'vocab', scatter_dimen...]
    all_to_all x1 -> x0, blocking collectives: 59.5 us -> none  [on_device(): lax.all_to_all(partial_rows, 'seq', split_axis=1, concat_axis=2, tiled=True)]
  transfers between devices with their start and end apart: 9 -> 1, of which waited for: 7 -> 1; matrix products, arithmetic and copies ran while one was open for 1% -> 9% of each run, Pallas kernels for 0% -> 21%
where the time goes in v3:
time: 228 us
  Pallas kernels  181 us (79%)
  local copies, waits for them, and re-layouts  26.1 us (11%)
  between operations  13.6 us (6%)
  other arithmetic  4.95 us (2%)
    pallas_call x4, Pallas kernels, call(): pl.pallas_call(kernel, out_shape=out, in_specs=in_specs or [vmem] * len(o...  181 us
    gather x1, local copies, waits for them, and re-layouts, on_device(): jnp.take(embed_table, jnp.clip(local_ids, 0, shard_rows - 1), axis=0)  12.1 us
    unnamed x10, local copies, waits for them, and re-layouts  5.72 us
  transfers between devices with their start and end apart: 1, of which 1 were waited for; matrix products, arithmetic and copies ran while one was open for 9% of the time, Pallas kernels for 21%

profile of v3, /device:TPU:480, one launch (start us, length us, event | category | flops | bytes accessed | tf_op | source)
XLA Modules:
  0.0 227.6 jit_solution(17901093503066547331)
XLA Ops:
  6.5 0.0 copy-start
  6.5 0.9 stack_reshape.6
  7.5 0.1 copy.23
  7.5 0.8 stack_reshape.7
  8.3 0.1 copy.24
  8.4 0.2 maximum_bitcast_fusion.1
  8.6 0.7 reshape.135.both_ref
  9.3 0.7 compare_select_fusion.2
  10.0 0.6 reshape.134.ids_ref
  10.6 0.9 copy.28
  11.5 0.9 copy.29
  12.4 0.9 copy.30
  13.2 0.9 copy.31
  14.2 0.1 copy.33
  14.3 17.4 %shard_map.145 = (s32[8,4,1,128]{3,2,1,0:T(1,128)}, bf16[4,32,128]{2,1,0:T(8,128)(2,1)}) custom-call(s32[1,128]{1,0:T(1,128)} %reshape.134.ids_ref, bf16[4,32,128]{2,1,0:T(8,128)(2,1)} %reshape.135.both_ref), custom_call_target="tpu_custom_call" | custom-call | tf_op jit(solution)/shard_map/pallas_call | solution.py:93
  31.7 1.4 pad_maximum_fusion
  33.1 0.0 all-gather.3.cloned.1.call-update
  33.2 1.8 reshape.143
  35.0 1.5 dynamic-slice_reduce_fusion
  36.5 0.8 copy.40
  37.3 0.1 clamp_reduce_fusion
  37.3 0.1 reshape.158
  37.5 0.1 min.24
  37.6 0.1 reshape.159
  37.8 12.1 %gather_fusion = bf16[4096,128]{1,0:T(8,128)(2,1)S(1)} fusion(bf16[8192,128]{1,0:T(8,128)(2,1)S(1)} %copy-done, s32[4096]{0:T(1024)S(1)} %broadcast_clamp_fusion), kind=kCustom, calls=%fused_computation | custom fusion | bytes 2113536 | tf_op jit(solution)/shard_map/jit(_take)/gather | solution.py:486
  49.9 2.5 %select_select_fusion.x_ref = bf16[2,4,8,64,128]{4,3,2,1,0:T(8,128)(2,1)} fusion(bf16[2,4,8,64,128]{4,3,2,1,0:T(8,128)(2,1)S(1)} %bitcast.48, pred[2,4,8,64]{3,2,1,0:T(8,128)(4,1)S(1)} %compare_and_fusion.1, pred[2,4,8,64]{3,2,1,0:T(8,128)(4,1)S(1)} %bitcast.61), kind=kLoop, calls=%fused_computation.1 | loop fusion | flops 1048576 | bytes 2105344 | tf_op jit(solution)/shard_map/jit(_where)/select_n | solution.py:487
  52.4 46.7 %shard_map.146 = (bf16[64,1024]{1,0:T(8,128)(2,1)}, bf16[2,4,64,1024]{3,2,1,0:T(8,128)(2,1)}) custom-call(bf16[2,4,8,64,128]{4,3,2,1,0:T(8,128)(2,1)} %select_select_fusion.x_ref), custom_call_target="tpu_custom_call" | custom-call | tf_op jit(solution)/shard_map/pallas_call | solution.py:93
  99.1 1.3 dynamic-slice_bitcast_fusion
  100.4 1.6 all-gather.3.cloned.1.call-done.weight_ref
  102.0 76.8 %shard_map.147 = bf16[2,4,64,1024]{3,2,1,0:T(8,128)(2,1)} custom-call(s32[2]{0:T(128)} %length_ref.2, bf16[512,1024]{1,0:T(8,128)(2,1)} %bitcast.49, bf16[64,1024]{1,0:T(8,128)(2,1)} %get-tuple-element.11.own_ref, f32[1,1024]{1,0:T(1,128)} %get-tuple-element.14.gain_ref, bf16[1024,640]{1,0:T(8,128)(2,1)} %all-gather.3.cloned.1.call-done.weight_ref, ...), custom_call_target="tpu_custom_call" | custom-call | tf_op jit(solution)/shard_map/pallas_call | solution.py:93
  178.9 40.4 %shard_map.148 = bf16[128,256]{1,0:T(8,128)(2,1)} custom-call(s32[2]{0:T(128)} %length_ref.3, bf16[512,1024]{1,0:T(8,128)(2,1)} %bitcast.47, f32[1,1024]{1,0:T(1,128)} %get-tuple-element.13.gain_ref, bf16[1024,640]{1,0:T(8,128)(2,1)} %all-gather.3.cloned.1.call-done.weight_ref, bf16[128,4096]{1,0:T(8,128)(2,1)} %out_ref.1), custom_call_target="tpu_custom_call" | custom-call | tf_op jit(solution)/shard_map/pallas_call | solution.py:93
  219.3 1.5 copy.43
  (13 shorter events, 0.1 us)
Async XLA Ops:
  6.5 31.2 %copy-start = (bf16[8192,128]{1,0:T(8,128)(2,1)S(1)}, bf16[8192,128]{1,0:T(8,128)(2,1)}, u32[]{:S(2)}) copy-start(bf16[8192,128]{1,0:T(8,128)(2,1)} %param.19) | copy-start | bytes 6291460
  6.5 95.5 %all-gather.3.cloned.1.call-start = ((), (), s32[]{:S(2)}) async-start(), calls=%async_computation | async-start | bytes 1474560 | tf_op jit(solution)/shard_map/all_gather | solution.py:480
  31.7 5.6 %copy-start.1 = (s32[8,4,1,128]{3,2,1,0:T(1,128)S(1)}, s32[8,4,1,128]{3,2,1,0:T(1,128)}, u32[]{:S(2)}) copy-start(s32[8,4,1,128]{3,2,1,0:T(1,128)} %get-tuple-element.9) | copy-start | bytes 49156
Sparse Core Ops, SparseCore 0:
  33.3 68.6 all-gather.2

commit v4 on v3

--- a/solution.py
+++ b/solution.py
@@ -59,25 +59,41 @@
     return copy
 
 
-def start_kernel(ids_ref, both_ref, all_ids, both_out, row_ids, own, y_s, y_r, z_s, z_r, b_s, b_r):
+def lanes_of(shape):
+    return lax.broadcasted_iota(jnp.int32, shape, 1)
+
+
+def by_head(left, right):
+    low = lanes_of(left.shape) < DH
+    return jnp.where(low, left, pltpu.roll(right, DH, 1)), jnp.where(low, pltpu.roll(left, DH, 1), right)
+
+
+def quarter_of(ref):
+    cols = ref.shape[1] // 32
+    starts = [pl.multiple_of((4 * k + place_on(LINE_Y)) * cols, cols) for k in range(8)]
+    return jnp.concatenate([ref[:, pl.ds(start, cols)] for start in starts], axis=1)
+
+
+def start_kernel(ids_ref, keys_ref, values_ref, all_ids, both_out, row_ids, both_ref, own, y_s, y_r, z_s, z_r, b_s, b_r):
     y, z = place_on(LINE_Y), place_on(LINE_Z)
     near, far = peers_on(LINE_Y), peers_on(LINE_Z)
     barrier = greet(near + far)
-    keep = [
-        pltpu.make_async_copy(ids_ref, row_ids.at[y], own.at[0]),
-        pltpu.make_async_copy(both_ref.at[y], both_out.at[y], own.at[1]),
-    ]
-    for copy in keep:
-        copy.start()
+    keep = pltpu.make_async_copy(ids_ref, row_ids.at[y], own.at[0])
+    keep.start()
+    for pair in range(2):
+        first, second = by_head(keys_ref[pair].astype(F32), values_ref[pair].astype(F32))
+        both_ref[2 * pair] = first.astype(BF16)
+        both_ref[2 * pair + 1] = second.astype(BF16)
+    both_out[y] = both_ref[y]
     pl.semaphore_wait(barrier, len(near + far))
     copies = [send(ids_ref, row_ids.at[y], near[k], y_s.at[k], y_r.at[k]) for k in range(3)]
     later = []
     for k in range(3):
         other = lax.rem(y + k + 1, 4)
         later.append(send(both_ref.at[other], both_out.at[y], near[k], b_s.at[k], b_r.at[k]))
-    for copy in keep + copies:
-        copy.wait()
-    last = pltpu.make_async_copy(row_ids, all_ids.at[z], own.at[2])
+    for copy in [keep] + copies:
+        copy.wait()
+    last = pltpu.make_async_copy(row_ids, all_ids.at[z], own.at[1])
     last.start()
     later += [send(row_ids, all_ids.at[z], far[k], z_s.at[k], z_r.at[k]) for k in range(7)]
     for copy in later + [last]:
@@ -151,9 +167,9 @@
     return sems(4) + sems(3) + [pltpu.SemaphoreType.DMA]
 
 
-def rows_kernel(x_ref, own_ref, all_ref, *refs):
+def rows_kernel(x_ref, both_ref, own_ref, all_ref, all_both, *refs):
     near, refs = refs[:8], refs[8:]
-    got, z_s, z_r, zh_s, zh_r = refs[:5]
+    got, z_s, z_r, zh_s, zh_r, b_s, b_r = refs[:7]
     half = near[3]
     z, zh = place_on(LINE_Z), place_on(LINE_ZH)
     v, s = lax.axis_index("vocab"), lax.axis_index("seq")
@@ -163,6 +179,8 @@
     devices = peers_on(LINE_CORE) + peers_on(LINE_X) + level + across
     barrier = greet(devices)
     pl.semaphore_wait(barrier, len(devices))
+    late = [send(both_ref, all_both.at[z], level[k], b_s.at[k], b_r.at[k]) for k in range(7)]
+    all_both[z] = both_ref[...]
     near_sum(x_ref, *near)
     copies = []
     for k in (4, 3, 5, 2, 6, 1, 7, 0):
@@ -176,19 +194,18 @@
     cols = got.shape[3]
     for k in range(8):
         own_ref[:, k * cols : (k + 1) * cols] = (got[0, k].astype(F32) + got[1, k].astype(F32)).astype(BF16)
-    spread(own_ref, all_ref, *refs[5:])
-
-
-def embed_rows(x, ident):
+    spread(own_ref, all_ref, *refs[7:])
+    for copy in late:
+        copy.wait()
+
+
+def embed_rows(x, both, ident):
     block = x.shape[2:]
     own = (block[1], block[0] * block[2])
-    out = (jax.ShapeDtypeStruct(own, BF16), jax.ShapeDtypeStruct((2, 4) + own, BF16))
-    scratch = near_sum_scratch(block) + [pltpu.VMEM((2,) + block, BF16)] + sems(7) + sems(8) + spread_scratch()
-    return call(rows_kernel, ident, out, scratch, (x,))
-
-
-def lanes_of(shape):
-    return lax.broadcasted_iota(jnp.int32, shape, 1)
+    out = tuple(jax.ShapeDtypeStruct(shape, BF16) for shape in (own, (2, 4) + own, (8,) + both.shape))
+    scratch = near_sum_scratch(block) + [pltpu.VMEM((2,) + block, BF16)]
+    scratch += sems(7) + sems(8) + sems(7) + spread_scratch()
+    return call(rows_kernel, ident, out, scratch, (x, both))
 
 
 def with_squares(product, squares, lane):
@@ -234,15 +251,19 @@
     def _():
         pl.semaphore_signal(barrier, inc=1, device_id=down, device_id_type=MESH)
 
-    row = emb_ref.shape[0] // 2
+    row, quarter = emb_ref.shape[0] // 2, emb_ref.shape[1]
+    gain = quarter_of(gain_ref)
+    weights = [weight_ref[:, k].reshape(quarter, 2 * DH) for k in range(3)]
     for pair in range(2):
         wide = emb_ref[pair * row : (pair + 1) * row].astype(F32)
         squares = jnp.sum(wide * wide, axis=-1, keepdims=True)
-        scaled = (wide * gain_ref[...]).astype(BF16)
+        scaled = (wide * gain).astype(BF16)
+        keys, values, queries = (jnp.dot(scaled, weight, preferred_element_type=F32) for weight in weights)
+        kv_heads = by_head(keys, values)
+        q_heads = (queries, pltpu.roll(queries, DH, 1))
         for head in range(2):
-            weight = weight_ref[:, head * 4 * DH : (head + 1) * 4 * DH]
-            product = jnp.dot(scaled, weight, preferred_element_type=F32)
-            blocks[2 * pair + head] = with_squares(product, squares, 3 * DH).astype(BF16)
+            blocks[2 * pair + head, :, : 2 * DH] = kv_heads[head].astype(BF16)
+            blocks[2 * pair + head, :, 2 * DH :] = with_squares(q_heads[head], squares, DH).astype(BF16)
     for k in range(1, 8):
 
         @pl.when(k > z)
@@ -313,9 +334,10 @@
 
     for copy in copies:
         copy.wait()
+    out_part = quarter_of(out_ref)
     for pair in range(2):
         context = got_ctx[2 * pair] + got_ctx[2 * pair + 1]
-        product = jnp.dot(context, out_ref[...], preferred_element_type=F32).astype(BF16)
+        product = jnp.dot(context, out_part, preferred_element_type=F32).astype(BF16)
         terms[pair] = product.reshape(terms.shape[1:])
     near_sum(terms, *near)
     send(half, got_zh, peers_on(LINE_ZH)[0], zh_s.at[0], zh_r.at[0]).wait()
@@ -346,7 +368,7 @@
     return call(functools.partial(self_kernel, width), ident, out, scratch, operands, specs)
 
 
-def cross_kernel(width, length_ref, after_ref, gain_ref, weight_ref, out_ref, result_ref, *refs):
+def cross_kernel(width, length_ref, after_ref, gain_ref, weight_ref, both_ref, out_ref, result_ref, *refs):
     blocks, got_y, ctx, got_ctx, terms, y_s, y_r, c_s, c_r, got_zh, zh_s, zh_r = refs[:12]
     near = refs[12:]
     half = near[3]
@@ -358,15 +380,17 @@
     row = after_ref.shape[0] // 2
     own = row // 4
     cols = 2 * DH
+    gain = quarter_of(gain_ref)
+    weight = weight_ref[:, 3].reshape(after_ref.shape[1], 2 * DH)
     share = pl.ds(pl.multiple_of((v // 2) * cols, cols), cols)
     for pair in range(2):
         wide = after_ref[pair * row : (pair + 1) * row].astype(F32)
         squares = jnp.sum(wide * wide, axis=-1, keepdims=True)
-        scaled = (wide * gain_ref[...]).astype(BF16)
+        scaled = (wide * gain).astype(BF16)
+        product = jnp.dot(scaled, weight, preferred_element_type=F32)
         for head in range(2):
-            weight = weight_ref[:, head * 4 * DH + 2 * DH : (head + 1) * 4 * DH]
-            product = jnp.dot(scaled, weight, preferred_element_type=F32)
-            blocks[2 * pair + head, :row] = with_squares(product, squares, 0).astype(BF16)
+            queries = pltpu.roll(product, DH, 1) if head else product
+            blocks[2 * pair + head, :row] = with_squares(queries, squares, DH).astype(BF16)
         for k in range(4):
             lower = pair * row + k * own
             blocks[k, row + pair * own : row + (pair + 1) * own] = after_ref[lower : lower + own, share]
@@ -378,9 +402,9 @@
     got_y[y] = blocks[y]
     for copy in copies:
         copy.wait()
-    query = pltpu.roll(scaled_sum(got_y, row, 0, width), DH, 1)
+    query = scaled_sum(got_y, row, DH, width)
     query = jnp.where(lanes_of(query.shape) < DH, query, 0.0).astype(BF16)
-    both = weight_ref[:, 8 * DH :]
+    both = both_ref[...]
     visible = lanes_of((row, both.shape[0])) < length_ref[y // 2]
     ctx[...] = attend(query, both, visible, lax.rem(y, 2)).reshape(ctx.shape)
     copies = []
@@ -408,7 +432,7 @@
         result_ref[:, lanes] = (residual + total[:, lanes]).astype(BF16)
 
 
-def cross_block(ident, width, length, after, gain, weights, out_weight):
+def cross_block(ident, width, length, after, gain, weights, both, out_weight):
     row = after.shape[0] // 2
     own = row // 4
     block = (2, 2 * own, width // 16)
@@ -423,8 +447,8 @@
         ]
         + sems(3) + sems(3) + [pltpu.VMEM(block[1:], BF16)] + sems(1) + near_sum_scratch(block)
     )
-    operands = (length, after, gain, weights, out_weight)
-    specs = [pl.BlockSpec(memory_space=pltpu.SMEM)] + [vmem] * 4
+    operands = (length, after, gain, weights, both, out_weight)
+    specs = [pl.BlockSpec(memory_space=pltpu.SMEM)] + [vmem] * 5
     out = jax.ShapeDtypeStruct(block[1:], BF16)
     return call(functools.partial(cross_kernel, width), ident, out, scratch, operands, specs)
 
@@ -448,55 +472,47 @@
 ):
     pairs, tokens = token_ids.shape
     vocab_index = lax.axis_index("vocab")
-    y_index = place_on(LINE_Y)
     n_y, n_z = LINE_Y[1], LINE_Z[1]
     width = self_gain.shape[0]
     quarter = width // n_y
     cols = embed_table.shape[1]
-    heads = 2
     row_tokens = pairs * n_y * tokens
     pieces = 8
     piece = row_tokens // pieces
 
+    same_y = [[z * n_y + y for z in range(n_z)] for y in range(n_y)]
+    weights = jnp.stack([key_weight, value_weight, query_weight, cross_query_weight])
+    weights = lax.all_gather(weights, "seq", axis_index_groups=same_y)
+
     ids = jnp.where(keep_mask != 0, token_ids, -1).reshape(1, pairs * tokens)
-    pos = cross_keys.shape[1]
-    both = jnp.stack(
-        [cross_keys.reshape(pairs, pos, heads, DH), cross_values.reshape(pairs, pos, heads, DH)], axis=3
-    )
-    both = both.transpose(0, 2, 1, 3, 4).reshape(n_y, pos, 2 * DH)
+    both_shape = (n_y, cross_keys.shape[1], 2 * DH)
     out = (
         jax.ShapeDtypeStruct((n_z, n_y) + ids.shape, ids.dtype),
-        jax.ShapeDtypeStruct(both.shape, BF16),
+        jax.ShapeDtypeStruct(both_shape, BF16),
     )
-    scratch = [pltpu.VMEM((n_y,) + ids.shape, ids.dtype), pltpu.SemaphoreType.DMA((3,))]
-    ids, both = call(start_kernel, 0, out, scratch + sems(3) + sems(7) + sems(3), (ids, both))
+    scratch = [
+        pltpu.VMEM((n_y,) + ids.shape, ids.dtype),
+        pltpu.VMEM(both_shape, BF16),
+        pltpu.SemaphoreType.DMA((2,)),
+    ]
+    operands = (ids, cross_keys, cross_values)
+    ids, both = call(start_kernel, 0, out, scratch + sems(3) + sems(7) + sems(3), operands)
     ids = ids.reshape(n_z, n_y, pairs, tokens).transpose(0, 2, 1, 3)
     ids = ids.reshape(n_z, pieces, piece).transpose(1, 0, 2).reshape(-1)
-
-    weights = jnp.stack([key_weight, value_weight, query_weight, cross_query_weight], axis=1)
-    weights = weights.reshape(cols, 4, heads, DH).transpose(0, 2, 1, 3).reshape(cols, heads * 4 * DH)
-    weights = jnp.concatenate([weights, both.reshape(n_y * pos, 2 * DH)], axis=1)
-    same_y = [[z * n_y + y for z in range(n_z)] for y in range(n_y)]
-    weights = lax.all_gather(weights, "seq", axis_index_groups=same_y)
-    weights = weights.reshape(n_z * cols, weights.shape[2])
 
     shard_rows = embed_table.shape[0]
     local_ids = ids - vocab_index * shard_rows
     inside = (local_ids >= 0) & (local_ids < shard_rows)
     picked = jnp.take(embed_table, jnp.clip(local_ids, 0, shard_rows - 1), axis=0)
     picked = jnp.where(inside[:, None], picked, jnp.zeros_like(picked))
-    own_rows, embedded = embed_rows(picked.reshape(2, 4, n_z, piece, cols), 1)
+    own_rows, embedded, both = embed_rows(picked.reshape(2, 4, n_z, piece, cols), both, 1)
+    both = both.reshape(-1, 2 * DH)
     embedded = embedded.reshape(row_tokens, quarter)
 
-    def quarter_of(values):
-        part = values.reshape(-1, n_z, n_y, cols)
-        return lax.dynamic_index_in_dim(part, y_index, 2, False).reshape(-1, quarter)
-
-    out_part = quarter_of(self_out_weight)
-    self_part, cross_part = quarter_of(self_gain), quarter_of(cross_gain)
-    after = self_block(2, width, target_length, embedded, own_rows, self_part, weights, out_part)
+    gains = [gain.reshape(1, width) for gain in (self_gain, cross_gain)]
+    after = self_block(2, width, target_length, embedded, own_rows, gains[0], weights, self_out_weight)
     after = after.reshape(row_tokens, quarter)
-    result = cross_block(3, width, source_length, after, cross_part, weights, cross_out_weight)
+    result = cross_block(3, width, source_length, after, gains[1], weights, both, cross_out_weight)
     return result.reshape(pairs, tokens, result.shape[1])
 
 

time: 228 us -> 215 us (0.943)
  local copies, waits for them, and re-layouts: 26.1 us -> 14.5 us
    unnamed x10 -> x3, local copies, waits for them, and re-layouts: 5.72 us -> 1.48 us
    reshape x4 -> x0, local copies, waits for them, and re-layouts: 3.97 us -> none  [the longest x1 1.79 us: quarter_of(): part = values.reshape(-1, n_z, n_y, cols)]
  transfers between devices with their start and end apart: 1 -> 1, of which waited for: 1 -> 0; matrix products, arithmetic and copies ran while one was open for 9% -> 8% of each run, Pallas kernels for 21% -> 31%
where the time goes in v4:
time: 215 us; the launch traced here: 214 us
  Pallas kernels  180 us (84%)
  local copies, waits for them, and re-layouts  14.5 us (7%)
  between operations  13.5 us (6%)
  other arithmetic  6.41 us (3%)
    pallas_call x4, Pallas kernels, call(): pl.pallas_call(kernel, out_shape=out, in_specs=in_specs or [vmem] * len(o...  180 us
    gather x1, local copies, waits for them, and re-layouts, on_device(): jnp.take(embed_table, jnp.clip(local_ids, 0, shard_rows - 1), axis=0)  12.1 us
  transfers between devices with their start and end apart: 1, of which 0 were waited for; matrix products, arithmetic and copies ran while one was open for 8% of the time, Pallas kernels for 31%

profile of v4, /device:TPU:480, one launch (start us, length us, event | category | flops | bytes accessed | tf_op | source)
XLA Modules:
  0.0 214.0 jit_solution(10430296825012819540)
XLA Ops:
  6.5 0.0 copy-start
  6.5 0.0 all-gather.3.cloned.1.call-start
  6.5 1.6 pad_maximum_fusion
  8.2 0.0 all-gather.3.cloned.1.call-update
  8.2 0.7 compare_select_fusion.2
  8.9 0.6 reshape.101.ids_ref
  9.5 17.4 %shard_map.145 = (s32[8,4,1,128]{3,2,1,0:T(1,128)}, bf16[4,32,128]{2,1,0:T(8,128)(2,1)}) custom-call(s32[1,128]{1,0:T(1,128)} %reshape.101.ids_ref, bf16[2,32,128]{2,1,0:T(8,128)(2,1)} %keys_ref.1, bf16[2,32,128]{2,1,0:T(8,128)(2,1)} %values_ref.1), custom_call_target="tpu_custom_call" | custom-call | tf_op jit(solution)/shard_map/pallas_call | solution.py:109
  26.9 0.8 clamp_reduce_fusion
  27.7 0.1 reshape.118
  27.8 0.1 min.24
  27.9 0.8 compare_and_fusion
  28.6 0.1 reshape.119
  28.8 0.0 copy-done
  28.8 12.1 %gather_fusion = bf16[4096,128]{1,0:T(8,128)(2,1)S(1)} fusion(bf16[8192,128]{1,0:T(8,128)(2,1)S(1)} %copy-done, s32[4096]{0:T(1024)S(1)} %broadcast_clamp_fusion), kind=kCustom, calls=%fused_computation | custom fusion | bytes 2113536 | tf_op jit(solution)/shard_map/jit(_take)/gather | solution.py:506
  40.9 2.5 %select_select_fusion.x_ref = bf16[2,4,8,64,128]{4,3,2,1,0:T(8,128)(2,1)} fusion(bf16[2,4,8,64,128]{4,3,2,1,0:T(8,128)(2,1)S(1)} %bitcast.38, pred[2,4,8,64]{3,2,1,0:T(8,128)(4,1)S(1)} %compare_and_fusion.1, pred[2,4,8,64]{3,2,1,0:T(8,128)(4,1)S(1)} %bitcast.45), kind=kLoop, calls=%fused_computation.1 | loop fusion | flops 1048576 | bytes 2105344 | tf_op jit(solution)/shard_map/jit(_where)/select_n | solution.py:507
  43.4 48.0 %shard_map.146 = (bf16[64,1024]{1,0:T(8,128)(2,1)}, bf16[2,4,64,1024]{3,2,1,0:T(8,128)(2,1)}, bf16[8,4,32,128]{3,2,1,0:T(8,128)(2,1)}) custom-call(bf16[2,4,8,64,128]{4,3,2,1,0:T(8,128)(2,1)} %select_select_fusion.x_ref, bf16[4,32,128]{2,1,0:T(8,128)(2,1)} %get-tuple-element.11.both_ref), custom_call_target="tpu_custom_call" | custom-call | tf_op jit(solution)/shard_map/pallas_call | solution.py:109
  91.5 0.0 all-gather.3.cloned.1.call-done
  91.5 76.7 %shard_map.147 = bf16[2,4,64,1024]{3,2,1,0:T(8,128)(2,1)} custom-call(s32[2]{0:T(128)} %length_ref.2, bf16[512,1024]{1,0:T(8,128)(2,1)} %bitcast.39, bf16[64,1024]{1,0:T(8,128)(2,1)} %get-tuple-element.13.own_ref, f32[1,4096]{1,0:T(1,128)} %bitcast.50, bf16[8,4,128,128]{3,2,1,0:T(8,128)(2,1)} %bitcast.35, bf16[128,4096]{1,0:T(8,128)(2,1)} %out_ref.2), custom_call_target="tpu_custom_call" | custom-call | tf_op jit(solution)/shard_map/pallas_call | solution.py:109
  168.2 37.5 %shard_map.148 = bf16[128,256]{1,0:T(8,128)(2,1)} custom-call(s32[2]{0:T(128)} %length_ref.3, bf16[512,1024]{1,0:T(8,128)(2,1)} %bitcast.37, f32[1,4096]{1,0:T(1,128)} %bitcast.51, bf16[8,4,128,128]{3,2,1,0:T(8,128)(2,1)} %bitcast.36, bf16[1024,128]{1,0:T(8,128)(2,1)} %bitcast.40, bf16[128,4096]{1,0:T(8,128)(2,1)} %out_ref.3), custom_call_target="tpu_custom_call" | custom-call | tf_op jit(solution)/shard_map/pallas_call | solution.py:109
  205.7 1.5 copy.26
  (6 shorter events, 0.1 us)
Async XLA Ops:
  6.5 22.2 %copy-start = (bf16[8192,128]{1,0:T(8,128)(2,1)S(1)}, bf16[8192,128]{1,0:T(8,128)(2,1)}, u32[]{:S(2)}) copy-start(bf16[8192,128]{1,0:T(8,128)(2,1)} %param.19) | copy-start | bytes 6291460
  6.5 85.0 %all-gather.3.cloned.1.call-start = ((), (), s32[]{:S(2)}) async-start(), calls=%async_computation | async-start | bytes 1179648 | tf_op jit(solution)/shard_map/all_gather | solution.py:485
Sparse Core Ops, SparseCore 0:
  9.4 68.3 all-gather.2

commit v5 on v4

--- a/solution.py
+++ b/solution.py
@@ -116,24 +116,66 @@
     )(*operands)
 
 
-def near_sum(x_ref, got_core, part, got_x, half, core_s, core_r, x_s, x_r):
+def half_pair(block):
+    return pltpu.VMEM((2, block[0] // 2) + tuple(block[1:]), BF16)
+
+
+def ring_far(line, source, relay, send_sem, recv_sem):
+    right, left = peer_of(line, 1)[0], peer_of(line, 3)[0]
+    rows = relay.shape[1]
+    return [
+        send(source.at[:rows], relay.at[0], right, send_sem.at[0], recv_sem.at[0]),
+        send(source.at[rows:], relay.at[1], left, send_sem.at[1], recv_sem.at[1]),
+    ]
+
+
+def ring_forward(line, far, relay, to_right, to_left, send_sem, recv_sem):
+    right, left = peer_of(line, 1)[0], peer_of(line, 3)[0]
+    far[0].wait()
+    first = send(relay.at[0], to_right, right, send_sem.at[4], recv_sem.at[4])
+    far[1].wait()
+    return [first, send(relay.at[1], to_left, left, send_sem.at[5], recv_sem.at[5])]
+
+
+def exchange_y(blocks, got, relay, send_sem, recv_sem):
+    y = place_on(LINE_Y)
+    before, behind = lax.rem(y + 3, 4), lax.rem(y + 1, 4)
+    right, left = peer_of(LINE_Y, 1)[0], peer_of(LINE_Y, 3)[0]
+    far = ring_far(LINE_Y, blocks.at[lax.rem(y + 2, 4)], relay, send_sem, recv_sem)
+    copies = [
+        send(blocks.at[behind], got.at[y], right, send_sem.at[2], recv_sem.at[2]),
+        send(blocks.at[before], got.at[y], left, send_sem.at[3], recv_sem.at[3]),
+    ]
+    got[y] = blocks[y]
+    rows = relay.shape[1]
+    copies += ring_forward(LINE_Y, far, relay, got.at[before, :rows], got.at[behind, rows:], send_sem, recv_sem)
+    for copy in copies:
+        copy.wait()
+
+
+def near_sum(x_ref, got_core, part, got_x, half, relay, core_s, core_r, x_s, x_r):
     core, place = place_on(LINE_CORE), place_on(LINE_X)
     twin, row = peers_on(LINE_CORE)[0], peers_on(LINE_X)
-    order = (1, 2, 3, 0)
+    order = (2, 1, 3, 0)
     core_copies = []
     for k, shift in enumerate(order):
         other = lax.rem(place + shift, 4)
         core_copies.append(send(x_ref.at[1 - core, other], got_core.at[other], twin, core_s.at[k], core_r.at[k]))
-    x_copies = []
+    copies = []
     for k, shift in enumerate(order):
         other = lax.rem(place + shift, 4)
         core_copies[k].wait()
         part[other] = (x_ref[core, other].astype(F32) + got_core[other].astype(F32)).astype(BF16)
-        if shift:
-            x_copies.append(send(part.at[other], got_x.at[k], row[k], x_s.at[k], x_r.at[k]))
+        if shift == 2:
+            far = ring_far(LINE_X, part.at[other], relay, x_s, x_r)
+        elif shift:
+            copies.append(send(part.at[other], got_x.at[shift - 1], row[shift - 1], x_s.at[k + 1], x_r.at[k + 1]))
+    half_rows = relay.shape[1]
+    copies += ring_forward(LINE_X, far, relay, got_x.at[1, :half_rows], got_x.at[1, half_rows:], x_s, x_r)
     total = part[place].astype(F32)
+    for copy in copies:
+        copy.wait()
     for k in range(3):
-        x_copies[k].wait()
         total = total + got_x[k].astype(F32)
     half[...] = total.astype(BF16)
 
@@ -144,7 +186,8 @@
         pltpu.VMEM((4,) + block, BF16),
         pltpu.VMEM((3,) + block, BF16),
         pltpu.VMEM(block, BF16),
-    ] + sems(4) + sems(3)
+        half_pair(block),
+    ] + sems(4) + sems(6)
 
 
 def spread(block, all_ref, core_s, core_r, x_s, x_r, local):
@@ -153,22 +196,40 @@
     keep = pltpu.make_async_copy(block, all_ref.at[core, place], local)
     keep.start()
     copies = [send(block, all_ref.at[core, place], twin, core_s.at[0], core_r.at[0])]
-    x_copies = [send(block, all_ref.at[core, place], row[k], x_s.at[k], x_r.at[k]) for k in range(3)]
-    for k in range(3):
-        x_copies[k].wait()
-        source = all_ref.at[core, lax.rem(place + 3 - k, 4)]
-        copies.append(send(source, source, twin, core_s.at[k + 1], core_r.at[k + 1]))
+    right, left = row[0], row[2]
+    rows = block.shape[0] // 2
+    upper, lower = slice(0, rows), slice(rows, 2 * rows)
+
+    def pass_on(source, member, part, target, k):
+        return send(source, all_ref.at[core, member, part], target, x_s.at[k], x_r.at[k])
+
+    first = pass_on(block.at[upper], place, upper, right, 0)
+    second = pass_on(block.at[lower], place, lower, left, 1)
+    from_left = pass_on(block.at[lower], place, lower, right, 2)
+    from_right = pass_on(block.at[upper], place, upper, left, 3)
+    before, behind = lax.rem(place + 3, 4), lax.rem(place + 1, 4)
+    first.wait()
+    far = [pass_on(all_ref.at[core, before, upper], before, upper, right, 4)]
+    second.wait()
+    far.append(pass_on(all_ref.at[core, behind, lower], behind, lower, left, 5))
+    for k, (member, needs) in enumerate(
+        ((before, [from_left]), (behind, [from_right]), (lax.rem(place + 2, 4), far))
+    ):
+        for copy in needs:
+            copy.wait()
+        whole = all_ref.at[core, member]
+        copies.append(send(whole, whole, twin, core_s.at[k + 1], core_r.at[k + 1]))
     for copy in copies:
         copy.wait()
     keep.wait()
 
 
 def spread_scratch():
-    return sems(4) + sems(3) + [pltpu.SemaphoreType.DMA]
+    return sems(4) + sems(6) + [pltpu.SemaphoreType.DMA]
 
 
 def rows_kernel(x_ref, both_ref, own_ref, all_ref, all_both, *refs):
-    near, refs = refs[:8], refs[8:]
+    near, refs = refs[:9], refs[9:]
     got, z_s, z_r, zh_s, zh_r, b_s, b_r = refs[:7]
     half = near[3]
     z, zh = place_on(LINE_Z), place_on(LINE_ZH)
@@ -233,8 +294,8 @@
 
 
 def self_kernel(width, length_ref, emb_ref, own_ref, gain_ref, weight_ref, out_ref, all_ref, *refs):
-    blocks, got_y, kv, got_ctx, terms, y_s, y_r, up_s, up_r, c_s, c_r, got_zh, piece, zh_s, zh_r = refs[:15]
-    near, far = refs[15:23], refs[23:]
+    blocks, got_y, kv, got_ctx, terms, y_s, y_r, up_s, up_r, c_s, c_r, got_zh, piece, zh_s, zh_r, relay = refs[:16]
+    near, far = refs[16:25], refs[25:]
     half = near[3]
     y, z = place_on(LINE_Y), place_on(LINE_Z)
     side = peers_on(LINE_Y)
@@ -278,13 +339,7 @@
     def _():
         pl.semaphore_wait(barrier, len(devices) + 1)
 
-    copies = []
-    for k in range(3):
-        other = lax.rem(y + k + 1, 4)
-        copies.append(send(blocks.at[other], got_y.at[y], side[k], y_s.at[k], y_r.at[k]))
-    got_y[y] = blocks[y]
-    for copy in copies:
-        copy.wait()
+    exchange_y(blocks, got_y, relay, y_s, y_r)
     qkv = scaled_sum(got_y, row, 3 * DH, width)
     kv[z] = qkv[:, : 2 * DH].astype(BF16)
     query = qkv[:, 2 * DH :]
@@ -358,9 +413,9 @@
             pltpu.VMEM((4, row, 2 * DH), BF16),
             pltpu.VMEM((2, 4) + piece, BF16),
         ]
-        + sems(3) + sems(14) + sems(3)
+        + sems(6) + sems(14) + sems(3)
         + [pltpu.VMEM(piece, BF16), pltpu.VMEM(piece, BF16)]
-        + sems(1) + near_sum_scratch(piece) + spread_scratch()
+        + sems(1) + [half_pair((row, 4 * DH))] + near_sum_scratch(piece) + spread_scratch()
     )
     operands = (length, embedded, own_rows, gain, weights, out_weight)
     specs = [pl.BlockSpec(memory_space=pltpu.SMEM)] + [vmem] * 5
@@ -369,8 +424,8 @@
 
 
 def cross_kernel(width, length_ref, after_ref, gain_ref, weight_ref, both_ref, out_ref, result_ref, *refs):
-    blocks, got_y, ctx, got_ctx, terms, y_s, y_r, c_s, c_r, got_zh, zh_s, zh_r = refs[:12]
-    near = refs[12:]
+    blocks, got_y, ctx, got_ctx, terms, y_s, y_r, c_s, c_r, got_zh, zh_s, zh_r, relay = refs[:13]
+    near = refs[13:]
     half = near[3]
     y, zh = place_on(LINE_Y), place_on(LINE_ZH)
     v = lax.axis_index("vocab")
@@ -395,13 +450,7 @@
             lower = pair * row + k * own
             blocks[k, row + pair * own : row + (pair + 1) * own] = after_ref[lower : lower + own, share]
     pl.semaphore_wait(barrier, len(devices))
-    copies = []
-    for k in range(3):
-        other = lax.rem(y + k + 1, 4)
-        copies.append(send(blocks.at[other], got_y.at[y], side[k], y_s.at[k], y_r.at[k]))
-    got_y[y] = blocks[y]
-    for copy in copies:
-        copy.wait()
+    exchange_y(blocks, got_y, relay, y_s, y_r)
     query = scaled_sum(got_y, row, DH, width)
     query = jnp.where(lanes_of(query.shape) < DH, query, 0.0).astype(BF16)
     both = both_ref[...]
@@ -445,7 +494,8 @@
             pltpu.VMEM((4, own, 2 * DH), BF16),
             pltpu.VMEM((2, 4) + block, BF16),
         ]
-        + sems(3) + sems(3) + [pltpu.VMEM(block[1:], BF16)] + sems(1) + near_sum_scratch(block)
+        + sems(6) + sems(3) + [pltpu.VMEM(block[1:], BF16)] + sems(1)
+        + [half_pair((row + 2 * own, 2 * DH))] + near_sum_scratch(block)
     )
     operands = (length, after, gain, weights, both, out_weight)
     specs = [pl.BlockSpec(memory_space=pltpu.SMEM)] + [vmem] * 5

time: 215 us -> 216 us (level)
  no operation moved by 1% of the time
where the time goes in v5:
time: 216 us; the launch traced here: 215 us
  Pallas kernels  180 us (83%)
  local copies, waits for them, and re-layouts  14.5 us (7%)
  between operations  13.5 us (6%)
  other arithmetic  6.41 us (3%)
    pallas_call x4, Pallas kernels, call(): pl.pallas_call(kernel, out_shape=out, in_specs=in_specs or [vmem] * len(o...  180 us
    gather x1, local copies, waits for them, and re-layouts, on_device(): jnp.take(embed_table, jnp.clip(local_ids, 0, shard_rows - 1), axis=0)  12.1 us
  transfers between devices with their start and end apart: 1, of which 0 were waited for; matrix products, arithmetic and copies ran while one was open for 8% of the time, Pallas kernels for 31%

profile of v5, /device:TPU:480, one launch (start us, length us, event | category | flops | bytes accessed | tf_op | source)
XLA Modules:
  0.0 214.6 jit_solution(6618683586499548559)
XLA Ops:
  6.5 0.0 copy-start
  6.5 0.0 all-gather.3.cloned.1.call-start
  6.5 1.6 pad_maximum_fusion
  8.2 0.0 all-gather.3.cloned.1.call-update
  8.2 0.7 compare_select_fusion.2
  8.9 0.6 reshape.101.ids_ref
  9.5 17.4 %shard_map.145 = (s32[8,4,1,128]{3,2,1,0:T(1,128)}, bf16[4,32,128]{2,1,0:T(8,128)(2,1)}) custom-call(s32[1,128]{1,0:T(1,128)} %reshape.101.ids_ref, bf16[2,32,128]{2,1,0:T(8,128)(2,1)} %keys_ref.1, bf16[2,32,128]{2,1,0:T(8,128)(2,1)} %values_ref.1), custom_call_target="tpu_custom_call" | custom-call | tf_op jit(solution)/shard_map/pallas_call | solution.py:109
  26.9 0.8 clamp_reduce_fusion
  27.7 0.1 reshape.118
  27.8 0.1 min.24
  27.9 0.8 compare_and_fusion
  28.6 0.1 reshape.119
  28.8 0.0 copy-done
  28.8 12.1 %gather_fusion = bf16[4096,128]{1,0:T(8,128)(2,1)S(1)} fusion(bf16[8192,128]{1,0:T(8,128)(2,1)S(1)} %copy-done, s32[4096]{0:T(1024)S(1)} %broadcast_clamp_fusion), kind=kCustom, calls=%fused_computation | custom fusion | bytes 2113536 | tf_op jit(solution)/shard_map/jit(_take)/gather | solution.py:556
  40.9 2.5 %select_select_fusion.x_ref = bf16[2,4,8,64,128]{4,3,2,1,0:T(8,128)(2,1)} fusion(bf16[2,4,8,64,128]{4,3,2,1,0:T(8,128)(2,1)S(1)} %bitcast.38, pred[2,4,8,64]{3,2,1,0:T(8,128)(4,1)S(1)} %compare_and_fusion.1, pred[2,4,8,64]{3,2,1,0:T(8,128)(4,1)S(1)} %bitcast.45), kind=kLoop, calls=%fused_computation.1 | loop fusion | flops 1048576 | bytes 2105344 | tf_op jit(solution)/shard_map/jit(_where)/select_n | solution.py:557
  43.4 48.3 %shard_map.146 = (bf16[64,1024]{1,0:T(8,128)(2,1)}, bf16[2,4,64,1024]{3,2,1,0:T(8,128)(2,1)}, bf16[8,4,32,128]{3,2,1,0:T(8,128)(2,1)}) custom-call(bf16[2,4,8,64,128]{4,3,2,1,0:T(8,128)(2,1)} %select_select_fusion.x_ref, bf16[4,32,128]{2,1,0:T(8,128)(2,1)} %get-tuple-element.11.both_ref), custom_call_target="tpu_custom_call" | custom-call | tf_op jit(solution)/shard_map/pallas_call | solution.py:109
  91.7 0.0 all-gather.3.cloned.1.call-done
  91.8 75.9 %shard_map.147 = bf16[2,4,64,1024]{3,2,1,0:T(8,128)(2,1)} custom-call(s32[2]{0:T(128)} %length_ref.2, bf16[512,1024]{1,0:T(8,128)(2,1)} %bitcast.39, bf16[64,1024]{1,0:T(8,128)(2,1)} %get-tuple-element.13.own_ref, f32[1,4096]{1,0:T(1,128)} %bitcast.50, bf16[8,4,128,128]{3,2,1,0:T(8,128)(2,1)} %bitcast.35, bf16[128,4096]{1,0:T(8,128)(2,1)} %out_ref.2), custom_call_target="tpu_custom_call" | custom-call | tf_op jit(solution)/shard_map/pallas_call | solution.py:109
  167.7 38.6 %shard_map.148 = bf16[128,256]{1,0:T(8,128)(2,1)} custom-call(s32[2]{0:T(128)} %length_ref.3, bf16[512,1024]{1,0:T(8,128)(2,1)} %bitcast.37, f32[1,4096]{1,0:T(1,128)} %bitcast.51, bf16[8,4,128,128]{3,2,1,0:T(8,128)(2,1)} %bitcast.36, bf16[1024,128]{1,0:T(8,128)(2,1)} %bitcast.40, bf16[128,4096]{1,0:T(8,128)(2,1)} %out_ref.3), custom_call_target="tpu_custom_call" | custom-call | tf_op jit(solution)/shard_map/pallas_call | solution.py:109
  206.3 1.5 copy.26
  (6 shorter events, 0.1 us)
Async XLA Ops:
  6.5 22.2 %copy-start = (bf16[8192,128]{1,0:T(8,128)(2,1)S(1)}, bf16[8192,128]{1,0:T(8,128)(2,1)}, u32[]{:S(2)}) copy-start(bf16[8192,128]{1,0:T(8,128)(2,1)} %param.19) | copy-start | bytes 6291460
  6.5 85.2 %all-gather.3.cloned.1.call-start = ((), (), s32[]{:S(2)}) async-start(), calls=%async_computation | async-start | bytes 1179648 | tf_op jit(solution)/shard_map/all_gather | solution.py:535
Sparse Core Ops, SparseCore 0:
  9.4 68.3 all-gather.2

commit v6 on v4

--- a/solution.py
+++ b/solution.py
@@ -116,26 +116,41 @@
     )(*operands)
 
 
-def near_sum(x_ref, got_core, part, got_x, half, core_s, core_r, x_s, x_r):
+def chunks_of(ref):
+    middle = ref.shape[0] // 2
+    return [slice(0, middle), slice(middle, 2 * middle)]
+
+
+def near_sum(x_ref, got_core, part, got_x, half, core_s, core_r, x_s, x_r, then=None):
     core, place = place_on(LINE_CORE), place_on(LINE_X)
     twin, row = peers_on(LINE_CORE)[0], peers_on(LINE_X)
     order = (1, 2, 3, 0)
+    chunks = chunks_of(half)
     core_copies = []
-    for k, shift in enumerate(order):
-        other = lax.rem(place + shift, 4)
-        core_copies.append(send(x_ref.at[1 - core, other], got_core.at[other], twin, core_s.at[k], core_r.at[k]))
+    for c, rows in enumerate(chunks):
+        for k, shift in enumerate(order):
+            other = lax.rem(place + shift, 4)
+            source, landing = x_ref.at[1 - core, other, rows], got_core.at[other, rows]
+            core_copies.append(send(source, landing, twin, core_s.at[4 * c + k], core_r.at[4 * c + k]))
     x_copies = []
-    for k, shift in enumerate(order):
-        other = lax.rem(place + shift, 4)
-        core_copies[k].wait()
-        part[other] = (x_ref[core, other].astype(F32) + got_core[other].astype(F32)).astype(BF16)
-        if shift:
-            x_copies.append(send(part.at[other], got_x.at[k], row[k], x_s.at[k], x_r.at[k]))
-    total = part[place].astype(F32)
-    for k in range(3):
-        x_copies[k].wait()
-        total = total + got_x[k].astype(F32)
-    half[...] = total.astype(BF16)
+    for c, rows in enumerate(chunks):
+        for k, shift in enumerate(order):
+            other = lax.rem(place + shift, 4)
+            core_copies[4 * c + k].wait()
+            term = x_ref[core, other, rows].astype(F32) + got_core[other, rows].astype(F32)
+            part[other, rows] = term.astype(BF16)
+            if shift:
+                index = 3 * c + k
+                landing = got_x.at[k, rows]
+                x_copies.append(send(part.at[other, rows], landing, row[k], x_s.at[index], x_r.at[index]))
+    for c, rows in enumerate(chunks):
+        total = part[place, rows].astype(F32)
+        for k in range(3):
+            x_copies[3 * c + k].wait()
+            total = total + got_x[k, rows].astype(F32)
+        half[rows] = total.astype(BF16)
+        if then is not None:
+            then(c, rows)
 
 
 def near_sum_scratch(block):
@@ -144,27 +159,37 @@
         pltpu.VMEM((4,) + block, BF16),
         pltpu.VMEM((3,) + block, BF16),
         pltpu.VMEM(block, BF16),
-    ] + sems(4) + sems(3)
-
-
-def spread(block, all_ref, core_s, core_r, x_s, x_r, local):
+    ] + sems(8) + sems(6)
+
+
+def spread(block, all_ref, core_s, core_r, x_s, x_r, local, fill=None):
     core, place = place_on(LINE_CORE), place_on(LINE_X)
     twin, row = peers_on(LINE_CORE)[0], peers_on(LINE_X)
+    chunks = chunks_of(block)
+    copies, x_copies = [], []
+    for c, rows in enumerate(chunks):
+        if fill is not None:
+            fill(c, rows)
+        landing = all_ref.at[core, place, rows]
+        for k in range(3):
+            index = 3 * c + k
+            x_copies.append(send(block.at[rows], landing, row[k], x_s.at[index], x_r.at[index]))
+        copies.append(send(block.at[rows], landing, twin, core_s.at[4 * c], core_r.at[4 * c]))
     keep = pltpu.make_async_copy(block, all_ref.at[core, place], local)
     keep.start()
-    copies = [send(block, all_ref.at[core, place], twin, core_s.at[0], core_r.at[0])]
-    x_copies = [send(block, all_ref.at[core, place], row[k], x_s.at[k], x_r.at[k]) for k in range(3)]
-    for k in range(3):
-        x_copies[k].wait()
-        source = all_ref.at[core, lax.rem(place + 3 - k, 4)]
-        copies.append(send(source, source, twin, core_s.at[k + 1], core_r.at[k + 1]))
+    for c, rows in enumerate(chunks):
+        for k in range(3):
+            x_copies[3 * c + k].wait()
+            source = all_ref.at[core, lax.rem(place + 3 - k, 4), rows]
+            index = 4 * c + k + 1
+            copies.append(send(source, source, twin, core_s.at[index], core_r.at[index]))
     for copy in copies:
         copy.wait()
     keep.wait()
 
 
 def spread_scratch():
-    return sems(4) + sems(3) + [pltpu.SemaphoreType.DMA]
+    return sems(8) + sems(6) + [pltpu.SemaphoreType.DMA]
 
 
 def rows_kernel(x_ref, both_ref, own_ref, all_ref, all_both, *refs):
@@ -339,10 +364,19 @@
         context = got_ctx[2 * pair] + got_ctx[2 * pair + 1]
         product = jnp.dot(context, out_part, preferred_element_type=F32).astype(BF16)
         terms[pair] = product.reshape(terms.shape[1:])
-    near_sum(terms, *near)
-    send(half, got_zh, peers_on(LINE_ZH)[0], zh_s.at[0], zh_r.at[0]).wait()
-    piece[...] = (own_ref[...].astype(F32) + (half[...].astype(F32) + got_zh[...].astype(F32))).astype(BF16)
-    spread(piece, all_ref, *far)
+    crossing = []
+
+    def cross_over(c, rows):
+        target = peers_on(LINE_ZH)[0]
+        crossing.append(send(half.at[rows], got_zh.at[rows], target, zh_s.at[c], zh_r.at[c]))
+
+    def fill(c, rows):
+        crossing[c].wait()
+        total = half[rows].astype(F32) + got_zh[rows].astype(F32)
+        piece[rows] = (own_ref[rows].astype(F32) + total).astype(BF16)
+
+    near_sum(terms, *near, then=cross_over)
+    spread(piece, all_ref, *far, fill=fill)
 
 
 def self_block(ident, width, length, embedded, own_rows, gain, weights, out_weight):
@@ -360,7 +394,7 @@
         ]
         + sems(3) + sems(14) + sems(3)
         + [pltpu.VMEM(piece, BF16), pltpu.VMEM(piece, BF16)]
-        + sems(1) + near_sum_scratch(piece) + spread_scratch()
+        + sems(2) + near_sum_scratch(piece) + spread_scratch()
     )
     operands = (length, embedded, own_rows, gain, weights, out_weight)
     specs = [pl.BlockSpec(memory_space=pltpu.SMEM)] + [vmem] * 5

time: 215 us -> 211 us (0.981)
  Pallas kernels: 180 us -> 176 us
    pallas_call x4, Pallas kernels: 180 us -> 176 us  [call(): pl.pallas_call(kernel, out_shape=out, in_specs=in_specs or [vmem] * len(o...]
where the time goes in v6:
time: 211 us; the launch traced here: 210 us
  Pallas kernels  176 us (83%)
  local copies, waits for them, and re-layouts  14.5 us (7%)
  between operations  13.5 us (6%)
  other arithmetic  6.41 us (3%)
    pallas_call x4, Pallas kernels, call(): pl.pallas_call(kernel, out_shape=out, in_specs=in_specs or [vmem] * len(o...  176 us
    gather x1, local copies, waits for them, and re-layouts, on_device(): jnp.take(embed_table, jnp.clip(local_ids, 0, shard_rows - 1), axis=0)  12.1 us
  transfers between devices with their start and end apart: 1, of which 0 were waited for; matrix products, arithmetic and copies ran while one was open for 8% of the time, Pallas kernels for 31%

profile of v6, /device:TPU:480, one launch (start us, length us, event | category | flops | bytes accessed | tf_op | source)
XLA Modules:
  0.0 210.0 jit_solution(17849487900506635549)
XLA Ops:
  6.5 0.0 copy-start
  6.5 0.0 all-gather.3.cloned.1.call-start
  6.5 1.6 pad_maximum_fusion
  8.2 0.0 all-gather.3.cloned.1.call-update
  8.2 0.7 compare_select_fusion.2
  8.9 0.6 reshape.101.ids_ref
  9.5 17.4 %shard_map.145 = (s32[8,4,1,128]{3,2,1,0:T(1,128)}, bf16[4,32,128]{2,1,0:T(8,128)(2,1)}) custom-call(s32[1,128]{1,0:T(1,128)} %reshape.101.ids_ref, bf16[2,32,128]{2,1,0:T(8,128)(2,1)} %keys_ref.1, bf16[2,32,128]{2,1,0:T(8,128)(2,1)} %values_ref.1), custom_call_target="tpu_custom_call" | custom-call | tf_op jit(solution)/shard_map/pallas_call | solution.py:109
  26.9 0.8 clamp_reduce_fusion
  27.7 0.1 reshape.118
  27.8 0.1 min.24
  27.9 0.8 compare_and_fusion
  28.6 0.1 reshape.119
  28.8 0.0 copy-done
  28.8 12.1 %gather_fusion = bf16[4096,128]{1,0:T(8,128)(2,1)S(1)} fusion(bf16[8192,128]{1,0:T(8,128)(2,1)S(1)} %copy-done, s32[4096]{0:T(1024)S(1)} %broadcast_clamp_fusion), kind=kCustom, calls=%fused_computation | custom fusion | bytes 2113536 | tf_op jit(solution)/shard_map/jit(_take)/gather | solution.py:540
  40.9 2.5 %select_select_fusion.x_ref = bf16[2,4,8,64,128]{4,3,2,1,0:T(8,128)(2,1)} fusion(bf16[2,4,8,64,128]{4,3,2,1,0:T(8,128)(2,1)S(1)} %bitcast.38, pred[2,4,8,64]{3,2,1,0:T(8,128)(4,1)S(1)} %compare_and_fusion.1, pred[2,4,8,64]{3,2,1,0:T(8,128)(4,1)S(1)} %bitcast.45), kind=kLoop, calls=%fused_computation.1 | loop fusion | flops 1048576 | bytes 2105344 | tf_op jit(solution)/shard_map/jit(_where)/select_n | solution.py:541
  43.4 47.9 %shard_map.146 = (bf16[64,1024]{1,0:T(8,128)(2,1)}, bf16[2,4,64,1024]{3,2,1,0:T(8,128)(2,1)}, bf16[8,4,32,128]{3,2,1,0:T(8,128)(2,1)}) custom-call(bf16[2,4,8,64,128]{4,3,2,1,0:T(8,128)(2,1)} %select_select_fusion.x_ref, bf16[4,32,128]{2,1,0:T(8,128)(2,1)} %get-tuple-element.11.both_ref), custom_call_target="tpu_custom_call" | custom-call | tf_op jit(solution)/shard_map/pallas_call | solution.py:109
  91.3 0.0 all-gather.3.cloned.1.call-done
  91.3 72.7 %shard_map.147 = bf16[2,4,64,1024]{3,2,1,0:T(8,128)(2,1)} custom-call(s32[2]{0:T(128)} %length_ref.2, bf16[512,1024]{1,0:T(8,128)(2,1)} %bitcast.39, bf16[64,1024]{1,0:T(8,128)(2,1)} %get-tuple-element.13.own_ref, f32[1,4096]{1,0:T(1,128)} %bitcast.50, bf16[8,4,128,128]{3,2,1,0:T(8,128)(2,1)} %bitcast.35, bf16[128,4096]{1,0:T(8,128)(2,1)} %out_ref.2), custom_call_target="tpu_custom_call" | custom-call | tf_op jit(solution)/shard_map/pallas_call | solution.py:109
  164.0 37.6 %shard_map.148 = bf16[128,256]{1,0:T(8,128)(2,1)} custom-call(s32[2]{0:T(128)} %length_ref.3, bf16[512,1024]{1,0:T(8,128)(2,1)} %bitcast.37, f32[1,4096]{1,0:T(1,128)} %bitcast.51, bf16[8,4,128,128]{3,2,1,0:T(8,128)(2,1)} %bitcast.36, bf16[1024,128]{1,0:T(8,128)(2,1)} %bitcast.40, bf16[128,4096]{1,0:T(8,128)(2,1)} %out_ref.3), custom_call_target="tpu_custom_call" | custom-call | tf_op jit(solution)/shard_map/pallas_call | solution.py:109
  201.6 1.5 copy.26
  (6 shorter events, 0.1 us)
Async XLA Ops:
  6.5 22.2 %copy-start = (bf16[8192,128]{1,0:T(8,128)(2,1)S(1)}, bf16[8192,128]{1,0:T(8,128)(2,1)}, u32[]{:S(2)}) copy-start(bf16[8192,128]{1,0:T(8,128)(2,1)} %param.19) | copy-start | bytes 6291460
  6.5 84.8 %all-gather.3.cloned.1.call-start = ((), (), s32[]{:S(2)}) async-start(), calls=%async_computation | async-start | bytes 1179648 | tf_op jit(solution)/shard_map/all_gather | solution.py:519
Sparse Core Ops, SparseCore 0:
  9.4 68.5 all-gather.2
